TPU v7x, 32 devices: a whole 2x2x4 slice. The times are simulated.
32 devices in a mesh: dp: 8 (over y, x, core), mp: 4 (over z).
Axes of the slice: x: 2, y: 2, z: 4, core: 2. Of those that a mesh axis runs over, the one named last changes fastest.
Arguments:
- token_ids: int32 [8, 1024], P('dp'), may hold values from 0 to 50303
- prompt_len: int32 [8], replicated, may hold values from 1 to 512, as said below
- example_len: int32 [8], replicated, may hold values from 512 to 1024, as said below
- embedding: bfloat16 [50304, 1024], P('mp'), may hold values from -6 to 6
- w_qkv: bfloat16 [1024, 3072], P(None, 'mp'), may hold values from -0.1875 to 0.1875
- w_out: bfloat16 [1024, 1024], P('mp'), may hold values from -0.75 to 0.75
- w_in: bfloat16 [1024, 4096], P(None, 'mp'), may hold values from -0.1875 to 0.1875
- b_in: float32 [4096], P('mp'), may hold values from -3 to 3
- w_down: bfloat16 [4096, 1024], P('mp'), may hold values from -0.09375 to 0.09375
- unembed: bfloat16 [1024, 50304], P('dp', 'mp'), may hold values from -0.1875 to 0.1875
- ln_gain: float32 [3, 1024], replicated, may hold values from 0.5 to 1.5
- ln_bias: float32 [3, 1024], replicated, may hold values from -3 to 3
- master: float32 [8, 1024, 128], P(None, ('dp', 'mp')), may hold values from -0.1875 to 0.1875
- first_moment: float32 [8, 1024, 128], P(None, ('dp', 'mp')), may hold values from -1.5258789e-05 to 1.5258789e-05
- second_moment: float32 [8, 1024, 128], P(None, ('dp', 'mp')), may hold values from 4.7683716e-14 to 7.6293946e-13
- eigen_bases: float32 [8, 128, 128], replicated, as said below
Outputs:
- mean_loss: float32 [], replicated
- grad_norm: float32 [], replicated
- new_first: float32 [8, 1024, 128], P(None, ('dp', 'mp'))
- new_second: float32 [8, 1024, 128], P(None, ('dp', 'mp'))
- new_master: float32 [8, 1024, 128], P(None, ('dp', 'mp'))
Inputs may be any that keep to these rules, and one draw needn't show every extreme that they name: `prompt_len`: each at most half of its example's length; the first example's is 512. `example_len`: the first example is 1024 tokens long. `eigen_bases`: each matrix is orthogonal.
All inputs are finite; a program needn't handle non-finite values.
Results may differ from a plain program's by a relative error of at most 0.0024.
Values may be sent and summed in bfloat16 or wider, within the bound.
A program may use at most 192 MiB of HBM per device.

v0:
```python
import jax
import jax.numpy as jnp
from jax import lax
from jax.sharding import PartitionSpec as P

D = 1024
HEADS = 16
R = 128
ADAM_STEP = 10
HD = 64
ROT = 16


HIGH_PRECISION = lax.Precision.HIGHEST
NORM_EPS = 1e-05
ROPE_BASE = 10000.0
CLIP_LIMIT = 0.01
LEARN_RATE = 0.02
BETA_FIRST = 0.9
BETA_SECOND = 0.999
ADAM_EPS = 1e-08
DECAY_RATE = 0.01


def merged(value, axis, join):
    pieces = jax.tree.map(lambda part: lax.all_gather(part, axis), value)
    head = jax.tree.map(lambda part: part[0], pieces)
    tail = jax.tree.map(lambda part: part[1:], pieces)
    running, _ = lax.scan(lambda running, section: (join(running, section), None), head, tail)
    return running


def layer_norm(values, gain, shift):
    centre = values - jnp.mean(values, -1, keepdims=True)
    spread = jnp.mean(centre * centre, -1, keepdims=True)
    return centre * lax.rsqrt(spread + NORM_EPS) * gain + shift


def norm_back(values, gain, shift, upstream):
    _, pullback = jax.vjp(lambda inputs: layer_norm(inputs, gain, shift), values)
    return pullback(upstream)[0]


def rope_tables(length):
    half = ROT // 2
    freqs = ROPE_BASE ** (-2.0 * jnp.arange(half, dtype=jnp.float32) / ROT)
    angles = jnp.arange(length, dtype=jnp.float32)[:, None] * freqs[None, :]
    return (jnp.cos(angles)[:, None, :], jnp.sin(angles)[:, None, :])


def rotate(field, cosine, sine):
    half = ROT // 2
    first = field[..., :half]
    second = field[..., half:ROT]
    return jnp.concatenate(
        [first * cosine - second * sine, second * cosine + first * sine, field[..., ROT:]], -1
    )


def rotate_back(upstream, cosine, sine):
    half = ROT // 2
    first = upstream[..., :half]
    second = upstream[..., half:ROT]
    return jnp.concatenate(
        [first * cosine + second * sine, second * cosine - first * sine, upstream[..., ROT:]], -1
    )


def masked_scores(queries, key_rows, start_row, stop_row):
    scores = jnp.einsum(
        "qhd,khd->hqk",
        queries[start_row:stop_row],
        key_rows[:stop_row],
        preferred_element_type=jnp.float32,
    ) * HD ** (-0.5)
    query_pos = start_row + jnp.arange(stop_row - start_row)[:, None]
    causal = jnp.arange(stop_row)[None, :] <= query_pos
    return jnp.where(causal[None], scores, -1e30)


def attend(queries, key_rows, value_rows):
    length = queries.shape[0]
    row_block = min(512, length)
    outputs = []
    spreads = []
    for start_row in range(0, length, row_block):
        stop_row = start_row + row_block
        scores = masked_scores(queries, key_rows, start_row, stop_row)
        top_score = jnp.max(scores, -1, keepdims=True)
        weights = jnp.exp(scores - top_score)
        row_total = jnp.sum(weights, -1, keepdims=True)
        probs = (weights / row_total).astype(jnp.bfloat16)
        outputs.append(
            jnp.einsum(
                "hqk,khd->qhd", probs, value_rows[:stop_row], preferred_element_type=jnp.float32
            )
        )
        spreads.append((top_score + jnp.log(row_total))[..., 0])
    return (jnp.concatenate(outputs, 0).astype(jnp.bfloat16), jnp.concatenate(spreads, 1))


def attend_back(queries, key_rows, value_rows, spreads, upstream):
    length = queries.shape[0]
    row_block = min(512, length)
    scaling = HD ** (-0.5)
    query_grads = []
    key_grad = jnp.zeros(key_rows.shape, jnp.float32)
    value_grad = jnp.zeros(value_rows.shape, jnp.float32)
    for start_row in range(0, length, row_block):
        stop_row = start_row + row_block
        scores = masked_scores(queries, key_rows, start_row, stop_row)
        probs = jnp.exp(scores - spreads[:, start_row:stop_row, None])
        grad_here = upstream[start_row:stop_row]
        prob_grad = jnp.einsum(
            "qhd,khd->hqk", grad_here, value_rows[:stop_row], preferred_element_type=jnp.float32
        )
        inner_sum = jnp.sum(probs * prob_grad, -1, keepdims=True)
        score_grad = (probs * (prob_grad - inner_sum)).astype(jnp.bfloat16)
        query_grads.append(
            jnp.einsum(
                "hqk,khd->qhd", score_grad, key_rows[:stop_row], preferred_element_type=jnp.float32
            )
            * scaling
        )
        key_grad = key_grad.at[:stop_row].add(
            jnp.einsum(
                "hqk,qhd->khd",
                score_grad,
                queries[start_row:stop_row],
                preferred_element_type=jnp.float32,
            )
            * scaling
        )
        value_grad = value_grad.at[:stop_row].add(
            jnp.einsum(
                "hqk,qhd->khd",
                probs.astype(jnp.bfloat16),
                grad_here,
                preferred_element_type=jnp.float32,
            )
        )
    return (jnp.concatenate(query_grads, 0), key_grad, value_grad)


def merge_stats(first, second):
    top_score = jnp.maximum(first[0], second[0])
    row_total = first[1] * jnp.exp(first[0] - top_score) + second[1] * jnp.exp(
        second[0] - top_score
    )
    return (top_score, row_total, first[2] + second[2])


def per_device(
    token_ids,
    prompt_len,
    example_len,
    embedding,
    w_qkv,
    w_out,
    w_in,
    b_in,
    w_down,
    unembed,
    ln_gain,
    ln_bias,
    master,
    first_moment,
    second_moment,
    eigen_bases,
):
    group_count = lax.axis_size("mp")
    group_index = lax.axis_index("mp")
    adapters = lax.all_gather(master.astype(jnp.bfloat16), ("dp", "mp"), axis=1, tiled=True)
    head_local = lax.all_gather(unembed, "dp", axis=0, tiled=True)
    examples, length = token_ids.shape
    width = embedding.shape[0]
    vocab_local = head_local.shape[1]
    rows = examples * length
    local_heads = HEADS // group_count
    group_width = local_heads * HD
    flat_ids = token_ids.reshape(rows)
    relative = flat_ids - group_index * width
    inside = (relative >= 0) & (relative < width)
    picked = jnp.where(
        inside[:, None], embedding[jnp.clip(relative, 0, width - 1)].astype(jnp.float32), 0.0
    )
    start_rows = lax.psum(picked.astype(jnp.bfloat16), "mp").astype(jnp.float32)
    leading_example = lax.axis_index("dp") * examples
    prompts = lax.dynamic_slice_in_dim(prompt_len, leading_example, examples)
    totals = lax.dynamic_slice_in_dim(example_len, leading_example, examples)
    position = jnp.arange(length)
    keep = (position[None, :] >= prompts[:, None] - 1) & (position[None, :] < totals[:, None] - 1)
    count = jnp.sum(example_len - prompt_len).astype(jnp.float32)
    row_weight = keep.reshape(rows).astype(jnp.float32) / count
    target = jnp.roll(token_ids, -1, axis=1).reshape(rows)
    normed_attn = layer_norm(start_rows, ln_gain[0], ln_bias[0]).astype(jnp.bfloat16)
    normed_ffn = layer_norm(start_rows, ln_gain[1], ln_bias[1]).astype(jnp.bfloat16)
    inner = jnp.dot(
        normed_attn,
        jnp.concatenate([adapters[0], adapters[1], adapters[2]], 1),
        preferred_element_type=jnp.float32,
    ).astype(jnp.bfloat16)
    base = jnp.dot(normed_attn, w_qkv, preferred_element_type=jnp.float32).reshape(
        rows, local_heads, 3, HD
    )
    adapter_rows = [
        lax.dynamic_slice_in_dim(
            adapters[3 + selector_index], group_index * group_width, group_width, 0
        )
        for selector_index in range(3)
    ]
    pre_parts = []
    for selector_index in range(3):
        extra = jnp.einsum(
            "lr,dr->ld",
            inner[:, selector_index * R : (selector_index + 1) * R],
            adapter_rows[selector_index],
            preferred_element_type=jnp.float32,
        )
        pre_parts.append(base[:, :, selector_index] + extra.reshape(rows, local_heads, HD))
    cosine, sine = rope_tables(length)
    queries = rotate(pre_parts[0].reshape(examples, length, local_heads, HD), cosine, sine).astype(
        jnp.bfloat16
    )
    key_rows = rotate(pre_parts[1].reshape(examples, length, local_heads, HD), cosine, sine).astype(
        jnp.bfloat16
    )
    value_rows = pre_parts[2].reshape(examples, length, local_heads, HD).astype(jnp.bfloat16)
    sample = 0
    context_here, spread_local = attend(queries[sample], key_rows[sample], value_rows[sample])
    spreads = [spread_local]
    context = context_here.reshape(rows, group_width)
    out_rows = lax.dynamic_slice_in_dim(adapters[6], group_index * group_width, group_width, 0)
    inner_out = jnp.dot(context, out_rows, preferred_element_type=jnp.float32).astype(jnp.bfloat16)
    hidden = jax.nn.gelu(
        jnp.dot(normed_ffn, w_in, preferred_element_type=jnp.float32) + b_in, approximate=False
    ).astype(jnp.bfloat16)
    partial_value = (
        jnp.dot(context, w_out, preferred_element_type=jnp.float32)
        + jnp.einsum("lr,dr->ld", inner_out, adapters[7], preferred_element_type=jnp.float32)
        + jnp.dot(hidden, w_down, preferred_element_type=jnp.float32)
    )
    resid = start_rows + lax.psum(partial_value, "mp")
    final_rows = layer_norm(resid, ln_gain[2], ln_bias[2]).astype(jnp.bfloat16)
    row_block = min(256, rows)
    blocks = rows // row_block
    vocab_ids = jnp.arange(vocab_local)[None, :]

    def block_stats(pieces):
        rows_here, target_here = pieces
        logits = jnp.dot(rows_here, head_local, preferred_element_type=jnp.float32)
        top_score = jnp.max(logits, -1)
        row_total = jnp.sum(jnp.exp(logits - top_score[:, None]), -1)
        hit = vocab_ids == (target_here - group_index * vocab_local)[:, None]
        return (top_score, row_total, jnp.sum(jnp.where(hit, logits, 0.0), -1))

    stats = lax.map(
        block_stats, (final_rows.reshape(blocks, row_block, D), target.reshape(blocks, row_block))
    )
    top_score, row_total, target_logit = merged(
        (stats[0].reshape(rows), stats[1].reshape(rows), stats[2].reshape(rows)), "mp", merge_stats
    )
    spread_all = top_score + jnp.log(row_total)
    local_loss = jnp.sum((spread_all - target_logit) * row_weight)

    def block_back(pieces):
        rows_here, target_here, spread_local, weight_here = pieces
        logits = jnp.dot(rows_here, head_local, preferred_element_type=jnp.float32)
        hit = (vocab_ids == (target_here - group_index * vocab_local)[:, None]).astype(jnp.float32)
        logit_grad = (
            (jnp.exp(logits - spread_local[:, None]) - hit) * weight_here[:, None]
        ).astype(jnp.bfloat16)
        return jnp.einsum("lv,dv->ld", logit_grad, head_local, preferred_element_type=jnp.float32)

    head_grad = lax.map(
        block_back,
        (
            final_rows.reshape(blocks, row_block, D),
            target.reshape(blocks, row_block),
            spread_all.reshape(blocks, row_block),
            row_weight.reshape(blocks, row_block),
        ),
    ).reshape(rows, D)
    branch_grad = norm_back(resid, ln_gain[2], ln_bias[2], lax.psum(head_grad, "mp")).astype(
        jnp.bfloat16
    )
    inner_out_grad = jnp.dot(branch_grad, adapters[7], preferred_element_type=jnp.float32).astype(
        jnp.bfloat16
    )
    grad_out_b = jnp.einsum("ld,lr->dr", branch_grad, inner_out, preferred_element_type=jnp.float32)
    grad_out_a = jnp.einsum(
        "ld,lr->dr", context, inner_out_grad, preferred_element_type=jnp.float32
    )
    context_grad = jnp.einsum(
        "ld,ed->le", branch_grad, w_out, preferred_element_type=jnp.float32
    ) + jnp.einsum("lr,dr->ld", inner_out_grad, out_rows, preferred_element_type=jnp.float32)
    context_grad = context_grad.astype(jnp.bfloat16).reshape(examples, length, local_heads, HD)
    sample = 0
    query_grad, key_grad, value_grad = attend_back(
        queries[sample], key_rows[sample], value_rows[sample], spreads[sample], context_grad[sample]
    )
    query_parts = [rotate_back(query_grad, cosine, sine)]
    key_parts = [rotate_back(key_grad, cosine, sine)]
    value_parts = [value_grad]
    pre_grads = [
        parts[0].reshape(rows, group_width).astype(jnp.bfloat16)
        for parts in (query_parts, key_parts, value_parts)
    ]
    complete_gradients = []
    local_grads = []
    for selector_index in range(3):
        projected_values = jnp.einsum(
            "ld,le->de", normed_attn, pre_grads[selector_index], preferred_element_type=jnp.float32
        )
        complete_gradients.append(
            jnp.dot(
                projected_values,
                adapter_rows[selector_index].astype(jnp.float32),
                precision=HIGH_PRECISION,
            )
        )
        local_grads.append(
            jnp.einsum(
                "ld,lr->dr",
                pre_grads[selector_index],
                inner[:, selector_index * R : (selector_index + 1) * R],
                preferred_element_type=jnp.float32,
            )
        )
    local_grads.append(grad_out_a)
    placed = lax.dynamic_update_slice(
        jnp.zeros((4, D, R), jnp.float32), jnp.stack(local_grads), (0, group_index * group_width, 0)
    )
    gradient = jnp.concatenate([jnp.stack(complete_gradients), placed, grad_out_b[None]], 0)
    owned = lax.psum_scatter(gradient, ("dp", "mp"), scatter_dimension=1, tiled=True)
    squares = jnp.sum(owned * owned)
    norm_squared = lax.psum(squares, ("dp", "mp"))
    mean_loss = lax.psum(local_loss, "dp")
    grad_norm = jnp.sqrt(norm_squared)
    clipped = owned * jnp.minimum(1.0, CLIP_LIMIT / grad_norm)
    rotated = jnp.einsum("mdr,mrs->mds", clipped, eigen_bases, precision=HIGH_PRECISION)
    new_first = BETA_FIRST * first_moment + (1.0 - BETA_FIRST) * rotated
    new_second = BETA_SECOND * second_moment + (1.0 - BETA_SECOND) * rotated * rotated
    normed = (
        new_first
        / (1.0 - BETA_FIRST**ADAM_STEP)
        / (jnp.sqrt(new_second / (1.0 - BETA_SECOND**ADAM_STEP)) + ADAM_EPS)
    )
    turned = jnp.einsum("mds,mrs->mdr", normed, eigen_bases, precision=HIGH_PRECISION)
    new_master = master - LEARN_RATE * (turned + DECAY_RATE * master)
    return (mean_loss, grad_norm, new_first, new_second, new_master)


def solution(mesh):
    placed = (
        P("dp", None),
        P(),
        P(),
        P("mp", None),
        P(None, "mp"),
        P("mp", None),
        P(None, "mp"),
        P("mp"),
        P("mp", None),
        P("dp", "mp"),
        P(),
        P(),
        P(None, ("dp", "mp"), None),
        P(None, ("dp", "mp"), None),
        P(None, ("dp", "mp"), None),
        P(),
    )
    return jax.shard_map(
        per_device,
        mesh=mesh,
        in_specs=placed,
        out_specs=(
            P(),
            P(),
            P(None, ("dp", "mp"), None),
            P(None, ("dp", "mp"), None),
            P(None, ("dp", "mp"), None),
        ),
        check_vma=False,
    )
```

profile of v0, /device:TPU:0, one launch (start us, length us, event | category | flops | bytes accessed | tf_op | source)
XLA Modules:
  0.0 1016.8 jit_solution(3470732560925565724)
XLA Ops:
  9.6 17.7 %gather_fusion = bf16[1024,1024]{1,0:T(8,128)(2,1)} fusion(bf16[12576,1024]{1,0:T(8,128)(2,1)} %param.37, s32[1024]{0:T(1024)S(1)} %broadcast_clamp_fusion), kind=kCustom, calls=%fused_computation | custom fusion | bytes 4198400 | tf_op jit(solution)/shard_map/gather | solution.py:185
  27.3 3.4 select_convert_fusion
  32.3 91.0 %all-reduce.6.cloned.1.call-done = bf16[1024,1024]{1,0:T(8,128)(2,1)} async-done(((bf16[1024,1024]{1,0:T(8,128)(2,1)}), bf16[1024,1024]{1,0:T(8,128)(2,1)}) %all-reduce.6.cloned.1.call-update) | async-done | bytes 2097168 | tf_op jit(solution)/shard_map/psum | solution.py:187
  128.5 3.5 fusion.191
  132.0 16.5 %fusion.56 = f32[1024,1024]{1,0:T(8,128)} fusion(bf16[1024,1024]{1,0:T(8,128)(2,1)S(1)} %copy-done, f32[1024]{0:T(1024)S(1)} %copy-done.75, bf16[1024,1024]{1,0:T(8,128)(2,1)} %param.40, bf16[1024,1024]{1,0:T(8,128)(2,1)} %all-reduce.6.cloned.1.call-done, f32[1024]{0:T(1024)S(1)} %bitcast.338, f32[1024]{0:T(1024)S(1)} %bitcast.337, ...), kind=kOutput, calls=%fused_computation.95 | convolution fusion | flops 4370464768 | bytes 10506240 | tf_op jit(solution)/shard_map/dot_general | solution.py:241
  150.1 3.0 convolution_convert_fusion
  167.2 3.8 add_add_fusion.1
  171.1 6.0 copy.47
  182.5 142.6 %all-reduce.8.cloned.1.call-done = f32[1024,1024]{1,0:T(8,128)} async-done(((f32[1024,1024]{1,0:T(8,128)}), f32[1024,1024]{1,0:T(8,128)}) %all-reduce.8.cloned.1.call-update) | async-done | bytes 4194320 | tf_op jit(solution)/shard_map/psum | solution.py:243
  325.2 2.8 fusion.182
  331.8 102.9 %while.54 = (s32[]{:T(128)}, f32[4,256]{1,0:T(4,128)S(1)}, f32[4,256]{1,0:T(4,128)S(1)}, f32[4,256]{1,0:T(4,128)S(1)}, bf16[4,256,1024]{2,1,0:T(8,128)(2,1)}, /*...) while((s32[]{:T(128)}, f32[4,256]{1,0:T(4,128)S(1)}, ...), condition=%wide.region_14.15_spmd.clone.clone, body=%wide.region_10.14_spmd.clone.sunk.clone | while | flops 6612762112 | bytes 52246120 | solution.py:257
  331.8 18.8 %fusion.255 = (f32[256]{0:T(256)S(1)}, f32[256,12576]{0,1:T(8,128)}) fusion(bf16[1024,12576]{1,0:T(8,128)(2,1)} %get-tuple-element.709, bf16[4,256,1024]{2,1,0:T(8,128)(2,1)} %get-tuple-element.708, s32[]{:T(128)} %get-tuple-element.696), kind=kOutput, calls=%fused_computation.294.clone.1.clone | convolution fusion | flops 6596665344 | bytes 39355904 | tf_op jit(solution)/shard_map/while/body/eval_jaxpr/dot_general | solution.py:251
  350.7 6.7 select_reduce_fusion.3
  357.6 18.9 %fusion.255 = (f32[256]{0:T(256)S(1)}, f32[256,12576]{0,1:T(8,128)}) fusion(bf16[1024,12576]{1,0:T(8,128)(2,1)} %get-tuple-element.709, bf16[4,256,1024]{2,1,0:T(8,128)(2,1)} %get-tuple-element.708, s32[]{:T(128)} %get-tuple-element.696), kind=kOutput, calls=%fused_computation.294.clone.1.clone | convolution fusion | flops 6596665344 | bytes 39355904 | tf_op jit(solution)/shard_map/while/body/eval_jaxpr/dot_general | solution.py:251
  376.5 6.7 select_reduce_fusion.3
  383.3 18.9 %fusion.255 = (f32[256]{0:T(256)S(1)}, f32[256,12576]{0,1:T(8,128)}) fusion(bf16[1024,12576]{1,0:T(8,128)(2,1)} %get-tuple-element.709, bf16[4,256,1024]{2,1,0:T(8,128)(2,1)} %get-tuple-element.708, s32[]{:T(128)} %get-tuple-element.696), kind=kOutput, calls=%fused_computation.294.clone.1.clone | convolution fusion | flops 6596665344 | bytes 39355904 | tf_op jit(solution)/shard_map/while/body/eval_jaxpr/dot_general | solution.py:251
  402.2 6.7 select_reduce_fusion.3
  409.1 18.8 %fusion.255 = (f32[256]{0:T(256)S(1)}, f32[256,12576]{0,1:T(8,128)}) fusion(bf16[1024,12576]{1,0:T(8,128)(2,1)} %get-tuple-element.709, bf16[4,256,1024]{2,1,0:T(8,128)(2,1)} %get-tuple-element.708, s32[]{:T(128)} %get-tuple-element.696), kind=kOutput, calls=%fused_computation.294.clone.1.clone | convolution fusion | flops 6596665344 | bytes 39355904 | tf_op jit(solution)/shard_map/while/body/eval_jaxpr/dot_general | solution.py:251
  427.9 6.7 select_reduce_fusion.3
  434.8 13.2 %all-gather = f32[4,1,1024]{2,1,0:T(1,128)S(1)} all-gather(f32[1,1,1024]{2,1,0:T(1,128)S(1)} %reshape.547), channel_id=1, replica_groups=mesh['dp'=8,'mp'=4] {'mp'}, dimensions={0}, use_global_device_ids=true | all-gather | bytes 20480 | tf_op jit(solution)/shard_map/all_gather | solution.py:26
  448.0 13.4 %all-gather.1 = f32[4,1,1024]{2,1,0:T(1,128)S(1)} all-gather(f32[1,1,1024]{2,1,0:T(1,128)S(1)} %reshape.549), channel_id=1, replica_groups=mesh['dp'=8,'mp'=4] {'mp'}, dimensions={0}, use_global_device_ids=true | all-gather | bytes 20480 | tf_op jit(solution)/shard_map/all_gather | solution.py:26
  461.4 13.2 %all-gather.2 = f32[4,1,1024]{2,1,0:T(1,128)S(1)} all-gather(f32[1,1,1024]{2,1,0:T(1,128)S(1)} %reshape.551), channel_id=1, replica_groups=mesh['dp'=8,'mp'=4] {'mp'}, dimensions={0}, use_global_device_ids=true | all-gather | bytes 20480 | tf_op jit(solution)/shard_map/all_gather | solution.py:26
  475.6 135.9 %while.55 = (s32[]{:T(128)}, f32[4,256,1024]{2,1,0:T(8,128)}, bf16[4,256,1024]{2,1,0:T(8,128)(2,1)}, bf16[1024,12576]{1,0:T(8,128)(2,1)}, f32[4,256]{1,0:T(4,128...) while((s32[]{:T(128)}, f32[4,256,1024]{2,1,0:T(8,128)}, ...), condition=%wide.region_21.22_spmd.clone.clone, body=%wide.region_20.21_spmd.clone.sunk.clone | while | flops 13206208512 | bytes 53487712 | solution.py:275
  475.6 34.0 %fusion.260 = f32[4,256,1024]{2,1,0:T(8,128)} fusion(f32[4,256,1024]{2,1,0:T(8,128)} %get-tuple-element.742, s32[]{:T(128)} %get-tuple-element.741, bf16[1024,12576]{1,0:T(8,128)(2,1)} %get-tuple-element.752, f32[256]{0:T(256)S(1)} %bitcast.331, s32[256]{0:T(256)S(1)} %bitcast.330, f32[256]{0:T(256)S(1)} %bitcast.332, ...), kind=kOutput, calls=%fused_computation.22.clone.1.clone | convolution fusion | flops 13206208512 | bytes 53481472 | tf_op jit(solution)/shard_map/while/body/eval_jaxpr/lv,dv->ld/dot_general | solution.py:273
  509.6 34.0 %fusion.260 = f32[4,256,1024]{2,1,0:T(8,128)} fusion(f32[4,256,1024]{2,1,0:T(8,128)} %get-tuple-element.742, s32[]{:T(128)} %get-tuple-element.741, bf16[1024,12576]{1,0:T(8,128)(2,1)} %get-tuple-element.752, f32[256]{0:T(256)S(1)} %bitcast.331, s32[256]{0:T(256)S(1)} %bitcast.330, f32[256]{0:T(256)S(1)} %bitcast.332, ...), kind=kOutput, calls=%fused_computation.22.clone.1.clone | convolution fusion | flops 13206208512 | bytes 53481472 | tf_op jit(solution)/shard_map/while/body/eval_jaxpr/lv,dv->ld/dot_general | solution.py:273
  543.6 33.9 %fusion.260 = f32[4,256,1024]{2,1,0:T(8,128)} fusion(f32[4,256,1024]{2,1,0:T(8,128)} %get-tuple-element.742, s32[]{:T(128)} %get-tuple-element.741, bf16[1024,12576]{1,0:T(8,128)(2,1)} %get-tuple-element.752, f32[256]{0:T(256)S(1)} %bitcast.331, s32[256]{0:T(256)S(1)} %bitcast.330, f32[256]{0:T(256)S(1)} %bitcast.332, ...), kind=kOutput, calls=%fused_computation.22.clone.1.clone | convolution fusion | flops 13206208512 | bytes 53481472 | tf_op jit(solution)/shard_map/while/body/eval_jaxpr/lv,dv->ld/dot_general | solution.py:273
  577.6 33.9 %fusion.260 = f32[4,256,1024]{2,1,0:T(8,128)} fusion(f32[4,256,1024]{2,1,0:T(8,128)} %get-tuple-element.742, s32[]{:T(128)} %get-tuple-element.741, bf16[1024,12576]{1,0:T(8,128)(2,1)} %get-tuple-element.752, f32[256]{0:T(256)S(1)} %bitcast.331, s32[256]{0:T(256)S(1)} %bitcast.330, f32[256]{0:T(256)S(1)} %bitcast.332, ...), kind=kOutput, calls=%fused_computation.22.clone.1.clone | convolution fusion | flops 13206208512 | bytes 53481472 | tf_op jit(solution)/shard_map/while/body/eval_jaxpr/lv,dv->ld/dot_general | solution.py:273
  612.2 153.3 %all-reduce.10.cloned.1.call-done = f32[1024,1024]{1,0:T(8,128)} async-done(((f32[1024,1024]{1,0:T(8,128)}), f32[1024,1024]{1,0:T(8,128)}) %all-reduce.10.cloned.1.call-update) | async-done | bytes 4194320 | tf_op jit(solution)/shard_map/psum | solution.py:284
  765.5 4.6 multiply_reduce_fusion.2
  803.2 148.2 %reduce-scatter.2.cloned.1.call-done = f32[8,32,128]{2,1,0:T(8,128)} async-done(((f32[8,1024,128]{2,1,0:T(8,128)}), f32[8,32,128]{2,1,0:T(8,128)}) %reduce-scatter.2.cloned.1.call-update) | async-done | bytes 131088 | tf_op jit(solution)/shard_map/reduce_scatter | solution.py:335
  952.9 12.4 %psum.37 = f32[]{:T(128)} all-reduce(f32[]{:T(128)} %get-tuple-element.415), channel_id=1, replica_groups=mesh['dp'=8,'mp'=4] {'dp'}, use_global_device_ids=true, to_apply=%region_19.20 | all-reduce | flops 1 | bytes 8 | tf_op jit(solution)/shard_map/psum | solution.py:338
  965.3 39.0 %psum.39 = f32[]{:T(128)} all-reduce(f32[]{:T(128)} %multiply_reduce_fusion.4), channel_id=1, replica_groups=mesh['dp'=8,'mp'=4] {'dp','mp'}, use_global_device_ids=true, to_apply=%region_29.30 | all-reduce | flops 1 | bytes 8 | tf_op jit(solution)/shard_map/psum | solution.py:337
  (319 shorter events, 70.4 us)
Async XLA Ops:
  8.0 124.0 %copy-start = (bf16[1024,1024]{1,0:T(8,128)(2,1)S(1)}, bf16[1024,1024]{1,0:T(8,128)(2,1)}, u32[]{:S(2)}) copy-start(bf16[1024,1024]{1,0:T(8,128)(2,1)} %param.42) | copy-start | bytes 6291460
  8.0 115.2 %all-reduce.6.cloned.1.call-start = ((), (), s32[]{:S(2)}) async-start(), calls=%async_computation.1 | async-start | bytes 4194304 | tf_op jit(solution)/shard_map/psum | solution.py:187
  30.7 117.8 %all-gather.6.cloned.1.call-start = ((), (), s32[]{:S(2)}) async-start(), calls=%async_computation.2 | async-start | bytes 2162688 | tf_op jit(solution)/shard_map/all_gather | solution.py:173
  31.5 293.7 %all-reduce.8.cloned.1.call-start = ((), (), s32[]{:S(2)}) async-start(), calls=%async_computation.3 | async-start | bytes 8388608 | tf_op jit(solution)/shard_map/psum | solution.py:243
  31.7 297.8 %copy-start.57 = (f32[1,1024]{1,0:T(1,128)}, f32[1,1024]{1,0:T(1,128)S(1)}, u32[]{:S(2)}) copy-start(f32[1,1024]{1,0:T(1,128)S(1)} %get-tuple-element.447) | copy-start | bytes 12292
  31.9 122.5 %copy-start.45 = (f32[1024,8]{0,1:T(8,128)}, f32[1024,8]{0,1:T(8,128)S(1)}, u32[]{:S(2)}) copy-start(f32[1024,8]{0,1:T(8,128)S(1)} %get-tuple-element.452) | copy-start | bytes 98308
  31.9 122.5 %copy-start.47 = (f32[1024,8]{0,1:T(8,128)}, f32[1024,8]{0,1:T(8,128)S(1)}, u32[]{:S(2)}) copy-start(f32[1024,8]{0,1:T(8,128)S(1)} %get-tuple-element.453) | copy-start | bytes 98308
  123.3 5.2 copy-start.74
  150.1 14.4 %copy-start.44 = (bf16[1,1024,128]{2,1,0:T(8,128)(2,1)}, bf16[1,1024,128]{2,1,0:T(8,128)(2,1)S(1)}, u32[]{:S(2)}) copy-start(bf16[1,1024,128]{2,1,0:T(8,128)(2,1)S(1)} %get-tuple-element.423) | copy-start | bytes 786436
  154.4 9.3 copy-start.14
  155.7 8.0 copy-start.8
  155.7 8.0 copy-start.64
  156.3 7.4 copy-start.66
  171.0 6.1 copy-start.63
  171.0 7.6 copy-start.77
  171.0 8.2 copy-start.76
  171.1 154.1 %copy-start.4 = (bf16[1024,1024]{1,0:T(8,128)(2,1)S(1)}, bf16[1024,1024]{1,0:T(8,128)(2,1)}, u32[]{:S(2)}) copy-start(bf16[1024,1024]{1,0:T(8,128)(2,1)} %all-reduce.6.cloned.1.call-done) | copy-start | bytes 6291460
  171.1 160.8 %all-gather.8.cloned.1.call-start = ((), (), s32[]{:S(2)}) async-start(), calls=%async_computation.4 | async-start | bytes 29196288 | tf_op jit(solution)/shard_map/all_gather | solution.py:174
  177.1 588.4 %all-reduce.10.cloned.1.call-start = ((), (), s32[]{:S(2)}) async-start(), calls=%async_computation.5 | async-start | bytes 8388608 | tf_op jit(solution)/shard_map/psum | solution.py:284
  611.4 154.0 %copy-start.5 = (bf16[1024,1024]{1,0:T(8,128)(2,1)S(1)}, bf16[1024,1024]{1,0:T(8,128)(2,1)}, u32[]{:S(2)}) copy-start(bf16[1024,1024]{1,0:T(8,128)(2,1)} %all-reduce.6.cloned.1.call-done) | copy-start | bytes 6291460
  611.5 154.0 %copy-start.56 = (f32[1024]{0:T(1024)S(1)}, f32[1024]{0:T(1024)}, u32[]{:S(2)}) copy-start(f32[1024]{0:T(1024)} %copy-done.55) | copy-start | bytes 12292
  611.5 154.0 %copy-start.58 = (f32[1,1024]{1,0:T(1,128)S(1)}, f32[1,1024]{1,0:T(1,128)}, u32[]{:S(2)}) copy-start(f32[1,1024]{1,0:T(1,128)} %copy-done.57) | copy-start | bytes 12292
  611.5 339.8 %reduce-scatter.2.cloned.1.call-start = ((), (), s32[]{:S(2)}) async-start(), calls=%async_computation.6 | async-start | bytes 4325376 | tf_op jit(solution)/shard_map/reduce_scatter | solution.py:335
  612.2 157.9 %copy-start.62 = (f32[1024]{0:T(1024)S(1)}, f32[1024]{0:T(1024)}, u32[]{:S(2)}) copy-start(f32[1024]{0:T(1024)} %copy-done.61) | copy-start | bytes 12292
  612.2 157.9 %copy-start.60 = (f32[1024]{0:T(1024)S(1)}, f32[1024]{0:T(1024)}, u32[]{:S(2)}) copy-start(f32[1024]{0:T(1024)} %copy-done.59) | copy-start | bytes 12292
  765.5 4.7 copy-start.7
  765.5 5.9 copy-start.12
  801.6 203.4 %copy-start.23 = (f32[8,128,128]{2,1,0:T(8,128)S(1)}, f32[8,128,128]{2,1,0:T(8,128)}, u32[]{:S(2)}) copy-start(f32[8,128,128]{2,1,0:T(8,128)} %param.49) | copy-start | bytes 1572868
  801.6 203.4 %copy-start.53 = (f32[8,32,128]{2,1,0:T(8,128)S(1)}, f32[8,32,128]{2,1,0:T(8,128)}, u32[]{:S(2)}) copy-start(f32[8,32,128]{2,1,0:T(8,128)} %param.48) | copy-start | bytes 393220
  801.6 203.4 %copy-start.54 = (f32[8,32,128]{2,1,0:T(8,128)S(1)}, f32[8,32,128]{2,1,0:T(8,128)}, u32[]{:S(2)}) copy-start(f32[8,32,128]{2,1,0:T(8,128)} %param.47) | copy-start | bytes 393220
  801.6 204.9 %copy-start.43 = (f32[8,32,128]{2,1,0:T(8,128)S(1)}, f32[8,32,128]{2,1,0:T(8,128)}, u32[]{:S(2)}) copy-start(f32[8,32,128]{2,1,0:T(8,128)} %param.46) | copy-start | bytes 393220
  801.6 206.5 %copy-start.1 = (bf16[1024,1024]{1,0:T(8,128)(2,1)S(1)}, bf16[1024,1024]{1,0:T(8,128)(2,1)}, u32[]{:S(2)}) copy-start(bf16[1024,1024]{1,0:T(8,128)(2,1)} %param.42) | copy-start | bytes 6291460
  (54 other events, 115.7 us)
Sparse Core Ops, SparseCore 0:
  30.9 92.3 all-reduce.5
  171.1 153.9 all-reduce.7
  611.6 153.8 all-reduce.9
Sparse Core Ops, SparseCore 1:
  34.7 99.2 all-gather.5
  177.2 127.2 all-gather.7
  803.3 148.0 reduce-scatter.1
where the time goes:
time: 1020 us
  waiting for transfers between devices  535 us (52%)
  matrix products  272 us (27%)
  blocking collectives  91.2 us (9%)
  other arithmetic  61.2 us (6%)
  local copies, waits for them, and re-layouts  36.4 us (4%)
  between operations  20.9 us (2%)
    psum x1, waiting for transfers between devices, per_device(): lax.psum(head_grad, 'mp')  153 us
    reduce_scatter x1, waiting for transfers between devices, per_device(): lax.psum_scatter(gradient, ('dp', 'mp'), scatter_dimension=1, tiled=True)  148 us
    psum x1, waiting for transfers between devices, per_device(): resid = start_rows + lax.psum(partial_value, 'mp')  143 us
    dot_general x4, matrix products, block_back(): jnp.einsum('lv,dv->ld', logit_grad, head_local, preferred_element_type=jn...  136 us
    psum x1, waiting for transfers between devices, per_device(): start_rows = lax.psum(picked.astype(jnp.bfloat16), 'mp').astype(jnp.float32)  91 us
    dot_general x4, matrix products, block_stats(): logits = jnp.dot(rows_here, head_local, preferred_element_type=jnp.float32)  75.4 us
    all_gather x3, blocking collectives, merged(): pieces = jax.tree.map(lambda part: lax.all_gather(part, axis), value)  39.8 us
    psum x1, blocking collectives, per_device(): norm_squared = lax.psum(squares, ('dp', 'mp'))  39 us
  transfers between devices with their start and end apart: 6, of which 4 were waited for; matrix products, arithmetic and copies ran while one was open for 4% of the time, Pallas kernels for 0%

commit v1 on v0

--- a/solution.py
+++ b/solution.py
@@ -1,7 +1,14 @@
+import functools
+
 import jax
 import jax.numpy as jnp
 from jax import lax
+from jax.experimental import pallas as pl
+from jax.experimental.pallas import tpu as pltpu
 from jax.sharding import PartitionSpec as P
+
+MESH = pl.DeviceIdType.MESH
+VMEM_LIMIT = 60 * 1024 * 1024
 
 D = 1024
 HEADS = 16
@@ -34,11 +41,6 @@
     centre = values - jnp.mean(values, -1, keepdims=True)
     spread = jnp.mean(centre * centre, -1, keepdims=True)
     return centre * lax.rsqrt(spread + NORM_EPS) * gain + shift
-
-
-def norm_back(values, gain, shift, upstream):
-    _, pullback = jax.vjp(lambda inputs: layer_norm(inputs, gain, shift), values)
-    return pullback(upstream)[0]
 
 
 def rope_tables(length):
@@ -148,6 +150,215 @@
         second[0] - top_score
     )
     return (top_score, row_total, first[2] + second[2])
+
+
+def line_chunk(index, size):
+    return pl.ds(pl.multiple_of(index * size, size), size)
+
+
+def greet_line(me, count):
+    barrier = pltpu.get_barrier_semaphore()
+
+    @pl.when(me > 0)
+    def _():
+        pl.semaphore_signal(
+            barrier, inc=1, device_id={"mp": jnp.maximum(me - 1, 0)}, device_id_type=MESH
+        )
+
+    @pl.when(me < count - 1)
+    def _():
+        pl.semaphore_signal(
+            barrier, inc=1, device_id={"mp": jnp.minimum(me + 1, count - 1)}, device_id_type=MESH
+        )
+
+    peers = jnp.where(me > 0, 1, 0) + jnp.where(me < count - 1, 1, 0)
+    pl.semaphore_wait(barrier, peers)
+
+
+def line_sum(count, chunk, own, wires, sems, prepare, emit):
+    me = lax.axis_index("mp")
+    from_low, from_high, to_high, to_low = wires
+    up_send, up_recv, down_send, down_recv = sems
+    length = own.shape[0]
+    chunks = length // chunk
+    above = jnp.minimum(me + 1, count - 1)
+    below = jnp.maximum(me - 1, 0)
+
+    def up_copy(index):
+        rows = line_chunk(index, chunk)
+        return pltpu.make_async_remote_copy(
+            src_ref=to_high.at[rows],
+            dst_ref=from_low.at[rows],
+            send_sem=up_send.at[index],
+            recv_sem=up_recv.at[index],
+            device_id={"mp": above},
+            device_id_type=MESH,
+        )
+
+    def down_copy(index):
+        rows = line_chunk(index, chunk)
+        return pltpu.make_async_remote_copy(
+            src_ref=to_low.at[rows],
+            dst_ref=from_high.at[rows],
+            send_sem=down_send.at[index],
+            recv_sem=down_recv.at[index],
+            device_id={"mp": below},
+            device_id_type=MESH,
+        )
+
+    greet_line(me, count)
+
+    @pl.when(me == 0)
+    def _():
+        from_low[...] = jnp.zeros_like(from_low)
+
+    @pl.when(me == count - 1)
+    def _():
+        from_high[...] = jnp.zeros_like(from_high)
+
+    def step(at, carry):
+        if prepare is not None:
+
+            @pl.when(at < chunks)
+            def _():
+                prepare(at)
+
+        up = at - LINE_LAG * me
+
+        @pl.when((up >= 0) & (up < chunks))
+        def _():
+            rows = line_chunk(up, chunk)
+
+            @pl.when(me > 0)
+            def _():
+                up_copy(up).wait_recv()
+
+            @pl.when(me < count - 1)
+            def _():
+                to_high[rows, :] = (
+                    from_low[rows, :].astype(jnp.float32) + own[rows, :].astype(jnp.float32)
+                ).astype(jnp.bfloat16)
+                up_copy(up).start()
+
+        down = at - LINE_LAG * (count - 1 - me)
+
+        @pl.when((down >= 0) & (down < chunks))
+        def _():
+            rows = line_chunk(down, chunk)
+
+            @pl.when(me < count - 1)
+            def _():
+                down_copy(down).wait_recv()
+
+            @pl.when(me > 0)
+            def _():
+                to_low[rows, :] = (
+                    from_high[rows, :].astype(jnp.float32) + own[rows, :].astype(jnp.float32)
+                ).astype(jnp.bfloat16)
+                down_copy(down).start()
+
+        ready = at - LINE_LAG * jnp.maximum(me, count - 1 - me)
+
+        @pl.when((ready >= 0) & (ready < chunks))
+        def _():
+            rows = line_chunk(ready, chunk)
+            total = (
+                from_low[rows, :].astype(jnp.float32)
+                + own[rows, :].astype(jnp.float32)
+                + from_high[rows, :].astype(jnp.float32)
+            )
+            emit(rows, total)
+
+        return carry
+
+    lax.fori_loop(0, chunks + LINE_LAG * (count - 1), step, 0)
+
+    def drain(index, carry):
+        @pl.when(me < count - 1)
+        def _():
+            up_copy(index).wait_send()
+
+        @pl.when(me > 0)
+        def _():
+            down_copy(index).wait_send()
+
+        return carry
+
+    lax.fori_loop(0, chunks, drain, 0)
+
+
+LINE_CHUNK = 32
+LINE_LAG = 3
+
+
+def line_scratch(length, width):
+    chunks = length // LINE_CHUNK
+    return [pltpu.VMEM((length, width), jnp.bfloat16)] * 4 + [
+        pltpu.SemaphoreType.DMA((chunks,))
+    ] * 4
+
+
+def line_call(kernel, name, collective_id, outs, scratch, operands, flops=0):
+    size = sum(o.size * o.dtype.itemsize for o in operands) + sum(
+        o.size * o.dtype.itemsize for o in outs
+    )
+    vmem = pl.BlockSpec(memory_space=pltpu.VMEM)
+    return pl.pallas_call(
+        kernel,
+        name=name,
+        out_shape=outs,
+        in_specs=[vmem] * len(operands),
+        out_specs=[vmem] * len(outs),
+        scratch_shapes=scratch,
+        compiler_params=pltpu.CompilerParams(
+            collective_id=collective_id, has_side_effects=True, vmem_limit_bytes=VMEM_LIMIT
+        ),
+        cost_estimate=pl.CostEstimate(
+            flops=flops, bytes_accessed=size + 100_000_000, transcendentals=0
+        ),
+    )(*operands)
+
+
+def start_kernel(count, part, gain, shift, rows_out, attn_out, ffn_out, *scratch):
+    def emit(rows, total):
+        rows_out[rows, :] = total.astype(jnp.bfloat16)
+        centre = total - jnp.mean(total, -1, keepdims=True)
+        spread = jnp.mean(centre * centre, -1, keepdims=True)
+        base = centre * lax.rsqrt(spread + NORM_EPS)
+        attn_out[rows, :] = (base * gain[0:1, :] + shift[0:1, :]).astype(jnp.bfloat16)
+        ffn_out[rows, :] = (base * gain[1:2, :] + shift[1:2, :]).astype(jnp.bfloat16)
+
+    line_sum(count, LINE_CHUNK, part, scratch[:4], scratch[4:], None, emit)
+
+
+def resid_kernel(count, part, start, gain, shift, resid_out, final_out, *scratch):
+    def emit(rows, total):
+        resid = start[rows, :].astype(jnp.float32) + total
+        resid_out[rows, :] = resid
+        normed = layer_norm(resid, gain[2:3, :], shift[2:3, :])
+        final_out[rows, :] = normed.astype(jnp.bfloat16)
+
+    line_sum(count, LINE_CHUNK, part, scratch[:4], scratch[4:], None, emit)
+
+
+def branch_kernel(count, part, resid, gain, out, *scratch):
+    def emit(rows, total):
+        values = resid[rows, :]
+        centre = values - jnp.mean(values, -1, keepdims=True)
+        spread = jnp.mean(centre * centre, -1, keepdims=True)
+        inverse = lax.rsqrt(spread + NORM_EPS)
+        normed = centre * inverse
+        up = total * gain[2:3, :]
+        out[rows, :] = (
+            inverse
+            * (
+                up
+                - jnp.mean(up, -1, keepdims=True)
+                - normed * jnp.mean(up * normed, -1, keepdims=True)
+            )
+        ).astype(jnp.bfloat16)
+
+    line_sum(count, LINE_CHUNK, part, scratch[:4], scratch[4:], None, emit)
 
 
 def per_device(
@@ -184,7 +395,16 @@
     picked = jnp.where(
         inside[:, None], embedding[jnp.clip(relative, 0, width - 1)].astype(jnp.float32), 0.0
     )
-    start_rows = lax.psum(picked.astype(jnp.bfloat16), "mp").astype(jnp.float32)
+    shape_low = jax.ShapeDtypeStruct((rows, D), jnp.bfloat16)
+    shape_wide = jax.ShapeDtypeStruct((rows, D), jnp.float32)
+    start_rows, normed_attn, normed_ffn = line_call(
+        functools.partial(start_kernel, group_count),
+        "start_rows",
+        0,
+        [shape_low] * 3,
+        line_scratch(rows, D),
+        [picked.astype(jnp.bfloat16), ln_gain, ln_bias],
+    )
     leading_example = lax.axis_index("dp") * examples
     prompts = lax.dynamic_slice_in_dim(prompt_len, leading_example, examples)
     totals = lax.dynamic_slice_in_dim(example_len, leading_example, examples)
@@ -193,8 +413,6 @@
     count = jnp.sum(example_len - prompt_len).astype(jnp.float32)
     row_weight = keep.reshape(rows).astype(jnp.float32) / count
     target = jnp.roll(token_ids, -1, axis=1).reshape(rows)
-    normed_attn = layer_norm(start_rows, ln_gain[0], ln_bias[0]).astype(jnp.bfloat16)
-    normed_ffn = layer_norm(start_rows, ln_gain[1], ln_bias[1]).astype(jnp.bfloat16)
     inner = jnp.dot(
         normed_attn,
         jnp.concatenate([adapters[0], adapters[1], adapters[2]], 1),
@@ -240,8 +458,14 @@
         + jnp.einsum("lr,dr->ld", inner_out, adapters[7], preferred_element_type=jnp.float32)
         + jnp.dot(hidden, w_down, preferred_element_type=jnp.float32)
     )
-    resid = start_rows + lax.psum(partial_value, "mp")
-    final_rows = layer_norm(resid, ln_gain[2], ln_bias[2]).astype(jnp.bfloat16)
+    resid, final_rows = line_call(
+        functools.partial(resid_kernel, group_count),
+        "resid_rows",
+        1,
+        [shape_wide, shape_low],
+        line_scratch(rows, D),
+        [partial_value.astype(jnp.bfloat16), start_rows, ln_gain, ln_bias],
+    )
     row_block = min(256, rows)
     blocks = rows // row_block
     vocab_ids = jnp.arange(vocab_local)[None, :]
@@ -281,8 +505,13 @@
             row_weight.reshape(blocks, row_block),
         ),
     ).reshape(rows, D)
-    branch_grad = norm_back(resid, ln_gain[2], ln_bias[2], lax.psum(head_grad, "mp")).astype(
-        jnp.bfloat16
+    (branch_grad,) = line_call(
+        functools.partial(branch_kernel, group_count),
+        "branch_rows",
+        2,
+        [shape_low],
+        line_scratch(rows, D),
+        [head_grad.astype(jnp.bfloat16), resid, ln_gain],
     )
     inner_out_grad = jnp.dot(branch_grad, adapters[7], preferred_element_type=jnp.float32).astype(
         jnp.bfloat16

time: 1020 us -> 801 us (0.79)
  waiting for transfers between devices: 535 us -> 149 us
  Pallas kernels: 0 us -> 187 us
  other arithmetic: 61.2 us -> 43.3 us
    psum x3 -> x0, waiting for transfers between devices: 387 us -> none  [the longest x1 153 us: per_device(): lax.psum(head_grad, 'mp')]
    pallas_call x0 -> x3, Pallas kernels: none -> 187 us  [line_call(): pl.pallas_call(kernel, name=name, out_shape=outs, in_specs=[vmem] * len(o...]
    reduce_sum x6 -> x0, other arithmetic: 14.6 us -> none  [the longest x3 6.89 us: layer_norm(): centre = values - jnp.mean(values, -1, keepdims=True)]
  transfers between devices with their start and end apart: 6 -> 3, of which waited for: 4 -> 1; matrix products, arithmetic and copies ran while one was open for 4% -> 9% of each run, Pallas kernels for 0% -> 17%
where the time goes in v1:
time: 801 us; the launch traced here: 795 us
  matrix products  274 us (34%)
  Pallas kernels  187 us (23%)
  waiting for transfers between devices  149 us (19%)
  blocking collectives  90.9 us (11%)
  other arithmetic  43.3 us (5%)
  local copies, waits for them, and re-layouts  32.1 us (4%)
  between operations  18.9 us (2%)
    pallas_call x3, Pallas kernels, line_call(): pl.pallas_call(kernel, name=name, out_shape=outs, in_specs=[vmem] * len(o...  187 us
    reduce_scatter x1, waiting for transfers between devices, per_device(): lax.psum_scatter(gradient, ('dp', 'mp'), scatter_dimension=1, tiled=True)  149 us
    dot_general x4, matrix products, block_back(): jnp.einsum('lv,dv->ld', logit_grad, head_local, preferred_element_type=jn...  135 us
    dot_general x4, matrix products, block_stats(): logits = jnp.dot(rows_here, head_local, preferred_element_type=jnp.float32)  75.4 us
    all_gather x3, blocking collectives, merged(): pieces = jax.tree.map(lambda part: lax.all_gather(part, axis), value)  39.6 us
    psum x1, blocking collectives, per_device(): norm_squared = lax.psum(squares, ('dp', 'mp'))  38.9 us
    reduce_sum x4, other arithmetic, block_stats(): return (top_score, row_total, jnp.sum(jnp.where(hit, logits, 0.0), -1))  26.9 us
    gather x1, local copies, waits for them, and re-layouts, per_device(): embedding[jnp.clip(relative, 0, width - 1)].astype(jnp.float32)  17.8 us
  transfers between devices with their start and end apart: 3, of which 1 were waited for; matrix products, arithmetic and copies ran while one was open for 9% of the time, Pallas kernels for 17%

profile of v1, /device:TPU:0, one launch (start us, length us, event | category | flops | bytes accessed | tf_op | source)
XLA Modules:
  0.0 795.3 jit_solution(1719681742609315711)
XLA Ops:
  9.0 5.6 copy.47
  19.9 17.8 %gather_fusion = bf16[1024,1024]{1,0:T(8,128)(2,1)} fusion(bf16[12576,1024]{1,0:T(8,128)(2,1)} %param.37, s32[1024]{0:T(1024)S(1)} %broadcast_clamp_fusion), kind=kCustom, calls=%fused_computation | custom fusion | bytes 4198400 | tf_op jit(solution)/shard_map/gather | solution.py:396
  37.7 3.4 select_convert_fusion.part
  41.0 70.4 %start_rows.1 = (bf16[1024,1024]{1,0:T(8,128)(2,1)}, bf16[1024,1024]{1,0:T(8,128)(2,1)}, bf16[1024,1024]{1,0:T(8,128)(2,1)}) custom-call(bf16[1024,1024]{1,0:T(8,128)(2,1)} %select_convert_fusion.part, f32[3,1024]{1,0:T(4,128)} %gain.5, f32[3,1024]{1,0:T(4,128)} %shift.3), custom_call_target="tpu_custom_call" | custom-call | bytes 108413184 | tf_op jit(solution)/shard_map/start_rows/pallas_call | solution.py:306
  112.2 5.5 fusion.169
  117.7 16.1 %fusion.41 = f32[1024,1024]{1,0:T(8,128)} fusion(bf16[1024,1024]{1,0:T(8,128)(2,1)S(1)} %copy-done, f32[1024]{0:T(1024)S(1)} %copy-done.51, bf16[1024,1024]{1,0:T(8,128)(2,1)} %get-tuple-element.326, bf16[1024,1024]{1,0:T(8,128)(2,1)} %param.40), kind=kOutput, calls=%fused_computation.73 | convolution fusion | flops 4364173312 | bytes 10489856 | tf_op jit(solution)/shard_map/dot_general | solution.py:459
  135.5 3.0 convolution_convert_fusion
  151.5 3.0 add_convert_fusion.part
  154.4 60.9 %resid_rows.1 = (f32[1024,1024]{1,0:T(8,128)}, bf16[1024,1024]{1,0:T(8,128)(2,1)}) custom-call(bf16[1024,1024]{1,0:T(8,128)(2,1)} %add_convert_fusion.part, bf16[1024,1024]{1,0:T(8,128)(2,1)} %get-tuple-element.327.start, f32[3,1024]{1,0:T(4,128)} %gain.5, f32[3,1024]{1,0:T(4,128)} %shift.3), custom_call_target="tpu_custom_call" | custom-call | bytes 110510336 | tf_op jit(solution)/shard_map/resid_rows/pallas_call | solution.py:306
  216.5 102.8 %while.54 = (s32[]{:T(128)}, f32[4,256]{1,0:T(4,128)S(1)}, f32[4,256]{1,0:T(4,128)S(1)}, f32[4,256]{1,0:T(4,128)S(1)}, bf16[4,256,1024]{2,1,0:T(8,128)(2,1)}, /*...) while((s32[]{:T(128)}, f32[4,256]{1,0:T(4,128)S(1)}, ...), condition=%wide.region_8.9_spmd.clone.clone, body=%wide.region_4.8_spmd.clone.sunk.clone | while | flops 6612762112 | bytes 52246120 | solution.py:481
  216.5 18.8 %fusion.234 = (f32[256]{0:T(256)S(1)}, f32[256,12576]{0,1:T(8,128)}) fusion(bf16[1024,12576]{1,0:T(8,128)(2,1)} %get-tuple-element.711, bf16[4,256,1024]{2,1,0:T(8,128)(2,1)} %get-tuple-element.710, s32[]{:T(128)} %get-tuple-element.698), kind=kOutput, calls=%fused_computation.264.clone.1.clone | convolution fusion | flops 6596665344 | bytes 39355904 | tf_op jit(solution)/shard_map/while/body/eval_jaxpr/dot_general | solution.py:475
  235.3 6.7 select_reduce_fusion.3
  242.2 18.8 %fusion.234 = (f32[256]{0:T(256)S(1)}, f32[256,12576]{0,1:T(8,128)}) fusion(bf16[1024,12576]{1,0:T(8,128)(2,1)} %get-tuple-element.711, bf16[4,256,1024]{2,1,0:T(8,128)(2,1)} %get-tuple-element.710, s32[]{:T(128)} %get-tuple-element.698), kind=kOutput, calls=%fused_computation.264.clone.1.clone | convolution fusion | flops 6596665344 | bytes 39355904 | tf_op jit(solution)/shard_map/while/body/eval_jaxpr/dot_general | solution.py:475
  261.1 6.7 select_reduce_fusion.3
  267.9 18.9 %fusion.234 = (f32[256]{0:T(256)S(1)}, f32[256,12576]{0,1:T(8,128)}) fusion(bf16[1024,12576]{1,0:T(8,128)(2,1)} %get-tuple-element.711, bf16[4,256,1024]{2,1,0:T(8,128)(2,1)} %get-tuple-element.710, s32[]{:T(128)} %get-tuple-element.698), kind=kOutput, calls=%fused_computation.264.clone.1.clone | convolution fusion | flops 6596665344 | bytes 39355904 | tf_op jit(solution)/shard_map/while/body/eval_jaxpr/dot_general | solution.py:475
  286.8 6.7 select_reduce_fusion.3
  293.7 18.9 %fusion.234 = (f32[256]{0:T(256)S(1)}, f32[256,12576]{0,1:T(8,128)}) fusion(bf16[1024,12576]{1,0:T(8,128)(2,1)} %get-tuple-element.711, bf16[4,256,1024]{2,1,0:T(8,128)(2,1)} %get-tuple-element.710, s32[]{:T(128)} %get-tuple-element.698), kind=kOutput, calls=%fused_computation.264.clone.1.clone | convolution fusion | flops 6596665344 | bytes 39355904 | tf_op jit(solution)/shard_map/while/body/eval_jaxpr/dot_general | solution.py:475
  312.5 6.7 select_reduce_fusion.3
  319.4 13.2 %all-gather = f32[4,1,1024]{2,1,0:T(1,128)S(1)} all-gather(f32[1,1,1024]{2,1,0:T(1,128)S(1)} %reshape.509), channel_id=1, replica_groups=mesh['dp'=8,'mp'=4] {'mp'}, dimensions={0}, use_global_device_ids=true | all-gather | bytes 20480 | tf_op jit(solution)/shard_map/all_gather | solution.py:33
  332.6 13.2 %all-gather.1 = f32[4,1,1024]{2,1,0:T(1,128)S(1)} all-gather(f32[1,1,1024]{2,1,0:T(1,128)S(1)} %reshape.511), channel_id=1, replica_groups=mesh['dp'=8,'mp'=4] {'mp'}, dimensions={0}, use_global_device_ids=true | all-gather | bytes 20480 | tf_op jit(solution)/shard_map/all_gather | solution.py:33
  345.9 13.2 %all-gather.2 = f32[4,1,1024]{2,1,0:T(1,128)S(1)} all-gather(f32[1,1,1024]{2,1,0:T(1,128)S(1)} %reshape.513), channel_id=1, replica_groups=mesh['dp'=8,'mp'=4] {'mp'}, dimensions={0}, use_global_device_ids=true | all-gather | bytes 20480 | tf_op jit(solution)/shard_map/all_gather | solution.py:33
  360.2 135.3 %while.55 = (s32[]{:T(128)}, bf16[4,256,1024]{2,1,0:T(8,128)(2,1)}, bf16[4,256,1024]{2,1,0:T(8,128)(2,1)}, bf16[1024,12576]{1,0:T(8,128)(2,1)}, f32[4,256]{1,0:T...) while((s32[]{:T(128)}, bf16[4,256,1024]{2,1,0:T(8,128)(2,1)}, ...), condition=%wide.region_15.16_spmd.clone.clone, body=%wide.region_14.15_spmd.clone.sunk.clone | while | flops 13206208512 | bytes 53487712 | solution.py:499
  360.3 33.8 %fusion.239 = bf16[4,256,1024]{2,1,0:T(8,128)(2,1)} fusion(bf16[4,256,1024]{2,1,0:T(8,128)(2,1)} %get-tuple-element.744, s32[]{:T(128)} %get-tuple-element.743, bf16[1024,12576]{1,0:T(8,128)(2,1)} %get-tuple-element.754, f32[256]{0:T(256)S(1)} %bitcast.322, s32[256]{0:T(256)S(1)} %bitcast.321, f32[256]{0:T(256)S(1)} %bitcast.323, ...), kind=kOutput, calls=%fused_computation.22.clone.1.clone | convolution fusion | flops 13206208512 | bytes 53481472 | tf_op jit(solution)/shard_map/while/body/eval_jaxpr/lv,dv->ld/dot_general | solution.py:497
  394.1 33.8 %fusion.239 = bf16[4,256,1024]{2,1,0:T(8,128)(2,1)} fusion(bf16[4,256,1024]{2,1,0:T(8,128)(2,1)} %get-tuple-element.744, s32[]{:T(128)} %get-tuple-element.743, bf16[1024,12576]{1,0:T(8,128)(2,1)} %get-tuple-element.754, f32[256]{0:T(256)S(1)} %bitcast.322, s32[256]{0:T(256)S(1)} %bitcast.321, f32[256]{0:T(256)S(1)} %bitcast.323, ...), kind=kOutput, calls=%fused_computation.22.clone.1.clone | convolution fusion | flops 13206208512 | bytes 53481472 | tf_op jit(solution)/shard_map/while/body/eval_jaxpr/lv,dv->ld/dot_general | solution.py:497
  427.9 33.8 %fusion.239 = bf16[4,256,1024]{2,1,0:T(8,128)(2,1)} fusion(bf16[4,256,1024]{2,1,0:T(8,128)(2,1)} %get-tuple-element.744, s32[]{:T(128)} %get-tuple-element.743, bf16[1024,12576]{1,0:T(8,128)(2,1)} %get-tuple-element.754, f32[256]{0:T(256)S(1)} %bitcast.322, s32[256]{0:T(256)S(1)} %bitcast.321, f32[256]{0:T(256)S(1)} %bitcast.323, ...), kind=kOutput, calls=%fused_computation.22.clone.1.clone | convolution fusion | flops 13206208512 | bytes 53481472 | tf_op jit(solution)/shard_map/while/body/eval_jaxpr/lv,dv->ld/dot_general | solution.py:497
  461.8 33.8 %fusion.239 = bf16[4,256,1024]{2,1,0:T(8,128)(2,1)} fusion(bf16[4,256,1024]{2,1,0:T(8,128)(2,1)} %get-tuple-element.744, s32[]{:T(128)} %get-tuple-element.743, bf16[1024,12576]{1,0:T(8,128)(2,1)} %get-tuple-element.754, f32[256]{0:T(256)S(1)} %bitcast.322, s32[256]{0:T(256)S(1)} %bitcast.321, f32[256]{0:T(256)S(1)} %bitcast.323, ...), kind=kOutput, calls=%fused_computation.22.clone.1.clone | convolution fusion | flops 13206208512 | bytes 53481472 | tf_op jit(solution)/shard_map/while/body/eval_jaxpr/lv,dv->ld/dot_general | solution.py:497
  495.6 55.9 %branch_rows.1 = bf16[1024,1024]{1,0:T(8,128)(2,1)} custom-call(bf16[1024,1024]{1,0:T(8,128)(2,1)} %bitcast.294, f32[1024,1024]{1,0:T(8,128)} %get-tuple-element.336.resid, f32[3,1024]{1,0:T(4,128)} %gain.5), custom_call_target="tpu_custom_call" | custom-call | bytes 108400896 | tf_op jit(solution)/shard_map/branch_rows/pallas_call | solution.py:306
  551.5 2.5 fusion.170
  562.7 2.6 multiply_reduce_fusion
  582.2 148.6 %reduce-scatter.2.cloned.1.call-done = f32[8,32,128]{2,1,0:T(8,128)} async-done(((f32[8,1024,128]{2,1,0:T(8,128)}), f32[8,32,128]{2,1,0:T(8,128)}) %reduce-scatter.2.cloned.1.call-update) | async-done | bytes 131088 | tf_op jit(solution)/shard_map/reduce_scatter | solution.py:564
  732.3 12.4 %psum.14 = f32[]{:T(128)} all-reduce(f32[]{:T(128)} %get-tuple-element.423), channel_id=1, replica_groups=mesh['dp'=8,'mp'=4] {'dp'}, use_global_device_ids=true, to_apply=%region_13.14 | all-reduce | flops 1 | bytes 8 | tf_op jit(solution)/shard_map/psum | solution.py:567
  744.7 38.9 %psum.15 = f32[]{:T(128)} all-reduce(f32[]{:T(128)} %multiply_reduce_fusion.2), channel_id=1, replica_groups=mesh['dp'=8,'mp'=4] {'dp','mp'}, use_global_device_ids=true, to_apply=%region_20.21 | all-reduce | flops 1 | bytes 8 | tf_op jit(solution)/shard_map/psum | solution.py:566
  (248 shorter events, 52.8 us)
Async XLA Ops:
  7.2 110.6 %copy-start = (bf16[1024,1024]{1,0:T(8,128)(2,1)S(1)}, bf16[1024,1024]{1,0:T(8,128)(2,1)}, u32[]{:S(2)}) copy-start(bf16[1024,1024]{1,0:T(8,128)(2,1)} %param.42) | copy-start | bytes 6291460
  7.2 126.7 %all-gather.6.cloned.1.call-start = ((), (), s32[]{:S(2)}) async-start(), calls=%async_computation.1 | async-start | bytes 2162688 | tf_op jit(solution)/shard_map/all_gather | solution.py:384
  8.9 5.8 copy-start.50
  8.9 7.1 copy-start.53
  9.0 7.7 copy-start.52
  9.0 207.6 %all-gather.8.cloned.1.call-start = ((), (), s32[]{:S(2)}) async-start(), calls=%async_computation.2 | async-start | bytes 29196288 | tf_op jit(solution)/shard_map/all_gather | solution.py:385
  14.7 716.1 %reduce-scatter.2.cloned.1.call-start = ((), (), s32[]{:S(2)}) async-start(), calls=%async_computation.3 | async-start | bytes 4325376 | tf_op jit(solution)/shard_map/reduce_scatter | solution.py:564
  111.8 27.5 %copy-start.38 = (f32[1024,8]{0,1:T(8,128)}, f32[1024,8]{0,1:T(8,128)S(1)}, u32[]{:S(2)}) copy-start(f32[1024,8]{0,1:T(8,128)S(1)} %get-tuple-element.454) | copy-start | bytes 98308
  111.8 27.5 %copy-start.40 = (f32[1024,8]{0,1:T(8,128)}, f32[1024,8]{0,1:T(8,128)S(1)}, u32[]{:S(2)}) copy-start(f32[1024,8]{0,1:T(8,128)S(1)} %get-tuple-element.455) | copy-start | bytes 98308
  112.2 5.5 copy-start.51
  135.4 13.3 %copy-start.37 = (bf16[1,1024,128]{2,1,0:T(8,128)(2,1)}, bf16[1,1024,128]{2,1,0:T(8,128)(2,1)S(1)}, u32[]{:S(2)}) copy-start(bf16[1,1024,128]{2,1,0:T(8,128)(2,1)S(1)} %get-tuple-element.431) | copy-start | bytes 786436
  135.4 3.1 copy-start.10
  135.5 3.4 copy-start.30
  135.5 3.4 copy-start.28
  139.9 6.1 copy-start.8
  140.9 4.3 copy-start.3
  143.3 3.3 copy-start.2
  495.6 55.9 %copy-start.16 = (bf16[256,1024]{1,0:T(8,128)(2,1)S(1)}, bf16[256,1024]{1,0:T(8,128)(2,1)}, u32[]{:S(2)}) copy-start(bf16[256,1024]{1,0:T(8,128)(2,1)} %param.39) | copy-start | bytes 1572868
  551.5 6.0 copy-start.4
  551.5 6.0 copy-start.9
  551.5 6.0 copy-start.49
  558.5 3.9 slice-start
  559.8 2.8 slice-start.1
  573.6 2.5 copy-start.29
  573.9 3.6 copy-start.33
  577.5 3.1 copy-start.6
  577.5 3.1 copy-start.23
  580.6 203.7 %copy-start.17 = (f32[8,128,128]{2,1,0:T(8,128)S(1)}, f32[8,128,128]{2,1,0:T(8,128)}, u32[]{:S(2)}) copy-start(f32[8,128,128]{2,1,0:T(8,128)} %param.49) | copy-start | bytes 1572868
  580.6 203.8 %copy-start.47 = (f32[8,32,128]{2,1,0:T(8,128)S(1)}, f32[8,32,128]{2,1,0:T(8,128)}, u32[]{:S(2)}) copy-start(f32[8,32,128]{2,1,0:T(8,128)} %param.48) | copy-start | bytes 393220
  580.6 203.8 %copy-start.48 = (f32[8,32,128]{2,1,0:T(8,128)S(1)}, f32[8,32,128]{2,1,0:T(8,128)}, u32[]{:S(2)}) copy-start(f32[8,32,128]{2,1,0:T(8,128)} %param.47) | copy-start | bytes 393220
  580.6 205.3 %copy-start.36 = (f32[8,32,128]{2,1,0:T(8,128)S(1)}, f32[8,32,128]{2,1,0:T(8,128)}, u32[]{:S(2)}) copy-start(f32[8,32,128]{2,1,0:T(8,128)} %param.46) | copy-start | bytes 393220
  580.6 206.9 %copy-start.1 = (bf16[1024,1024]{1,0:T(8,128)(2,1)S(1)}, bf16[1024,1024]{1,0:T(8,128)(2,1)}, u32[]{:S(2)}) copy-start(bf16[1024,1024]{1,0:T(8,128)(2,1)} %param.42) | copy-start | bytes 6291460
  (27 other events, 46.2 us)
Sparse Core Ops, SparseCore 0:
  11.5 62.7 all-gather.5
  76.1 127.0 all-gather.7
  582.3 148.4 reduce-scatter.1

commit v2 on v1

--- a/solution.py
+++ b/solution.py
@@ -359,6 +359,241 @@
         ).astype(jnp.bfloat16)
 
     line_sum(count, LINE_CHUNK, part, scratch[:4], scratch[4:], None, emit)
+
+
+def fold_kernel(splits, count, *refs):
+    fulls = refs[0:4]
+    groups = refs[4:8]
+    losses, master, first, second, bases = refs[8:13]
+    loss_out, norm_out, first_out, second_out, master_out = refs[13:18]
+    scratch = refs[18:]
+    sends = scratch[0:splits]
+    recvs = scratch[splits : 2 * splits]
+    keeps = scratch[2 * splits : 3 * splits]
+    (line_send, line_recv, turn_send, turn_recv, note_send, note_recv, tell_send, tell_recv) = scratch[
+        3 * splits : 3 * splits + 8
+    ]
+    (half_out, half_in, line_out, line_in, turn_out, turn_in, note_out, note_in, tell_out, tell_in) = (
+        scratch[3 * splits + 8 :]
+    )
+    shards = 2**splits
+    me = lax.axis_index("dp")
+    lane = lax.axis_index("mp")
+    full_rows = fulls[0].shape[0] // shards
+    group_rows = groups[0].shape[0] // shards
+    own_rows = full_rows // count
+    bits = [(me // 2**k) % 2 for k in range(splits)]
+    mates = [me + 2**k * (1 - 2 * bits[k]) for k in range(splits)]
+    peers = [lax.rem(lane + offset, count) for offset in range(count)]
+    spot = lane * shards + me
+    goal = (spot // count, lax.rem(spot, count))
+    place = me * count + lane
+    origin = (lax.rem(place, shards), place // shards)
+    moved = spot != place
+
+    barrier = pltpu.get_barrier_semaphore()
+    for mate in mates:
+        pl.semaphore_signal(barrier, inc=1, device_id={"dp": mate, "mp": lane}, device_id_type=MESH)
+    for peer in peers[1:]:
+        pl.semaphore_signal(barrier, inc=1, device_id={"dp": me, "mp": peer}, device_id_type=MESH)
+
+    @pl.when(moved)
+    def _():
+        for device in (goal, origin):
+            pl.semaphore_signal(
+                barrier, inc=1, device_id={"dp": device[0], "mp": device[1]}, device_id_type=MESH
+            )
+
+    pl.semaphore_wait(barrier, splits + count - 1 + jnp.where(moved, 2, 0))
+
+    def remote(src, dst, out_sem, in_sem, device):
+        return pltpu.make_async_remote_copy(
+            src_ref=src,
+            dst_ref=dst,
+            send_sem=out_sem,
+            recv_sem=in_sem,
+            device_id={"dp": device[0], "mp": device[1]},
+            device_id_type=MESH,
+        )
+
+    def piece(index):
+        whole = pl.ds(pl.multiple_of(index * full_rows, full_rows), full_rows)
+        part = pl.ds(pl.multiple_of(index * group_rows, group_rows), group_rows)
+        return jnp.concatenate(
+            [ref[whole, :] for ref in fulls] + [ref[part, :] for ref in groups], 0
+        )
+
+    started = []
+    current = piece
+    for k in range(splits):
+        half = shards >> (k + 1)
+        for i in range(half):
+            sends[k][i] = current(2 * i + 1 - bits[k]).astype(jnp.bfloat16)
+        copy = remote(sends[k], recvs[k], half_out.at[k], half_in.at[k], (mates[k], lane))
+        copy.start()
+        started.append(copy)
+        for i in range(half):
+            keeps[k][i] = current(2 * i + bits[k])
+        copy.wait_recv()
+        current = functools.partial(
+            lambda kept, came, i: kept[i] + came[i].astype(jnp.float32), keeps[k], recvs[k]
+        )
+    final = keeps[splits - 1]
+    final[0] = current(0)
+
+    def chosen(peer):
+        return jnp.concatenate(
+            [
+                final[
+                    0,
+                    pl.ds(pl.multiple_of(a * full_rows + peer * own_rows, own_rows), own_rows),
+                    :,
+                ]
+                for a in range(4)
+            ],
+            0,
+        )
+
+    turn_send[...] = final[0, 4 * full_rows :, :].astype(jnp.bfloat16)
+    turn = remote(turn_send, turn_recv, turn_out, turn_in, goal)
+
+    @pl.when(moved)
+    def _():
+        turn.start()
+
+    for offset in range(1, count):
+        line_send[offset] = chosen(peers[offset]).astype(jnp.bfloat16)
+        copy = remote(
+            line_send.at[offset],
+            line_recv.at[offset],
+            line_out.at[offset],
+            line_in.at[offset],
+            (me, peers[offset]),
+        )
+        copy.start()
+        started.append(copy)
+    total = chosen(lane)
+
+    @pl.when(moved)
+    def _():
+        turn.wait()
+
+    @pl.when(jnp.logical_not(moved))
+    def _():
+        turn_recv[...] = turn_send[...]
+
+    for copy in started[splits:]:
+        copy.wait_recv()
+    for offset in range(1, count):
+        total = total + line_recv[offset].astype(jnp.float32)
+    part = turn_recv[...].astype(jnp.float32)
+
+    column = lax.broadcasted_iota(jnp.int32, (8, 128), 1)
+    row = lax.broadcasted_iota(jnp.int32, (8, 128), 0)
+    squares = jnp.sum(total * total) + jnp.sum(part * part)
+    spot_norm = (row == 0) & (column == 0)
+    spot_loss = (row == 0) & (column == 1)
+    note = jnp.where(spot_norm, squares, 0.0) + jnp.where(spot_loss, jnp.sum(losses[...]), 0.0)
+
+    def rows_of(index):
+        source, slot = (total, (0, 1, 2, 7).index(index)) if index in (0, 1, 2, 7) else (
+            part,
+            index - 3,
+        )
+        return source[slot * own_rows : (slot + 1) * own_rows, :]
+
+    turned = [
+        jnp.dot(
+            rows_of(m), bases[m], precision=HIGH_PRECISION, preferred_element_type=jnp.float32
+        )
+        for m in range(8)
+    ]
+    for k in range(splits):
+        note_send[k] = note
+        copy = remote(
+            note_send.at[k], note_recv.at[k], note_out.at[k], note_in.at[k], (mates[k], lane)
+        )
+        copy.start()
+        started.append(copy)
+        copy.wait_recv()
+        note = note + note_recv[k]
+    tell_send[...] = note
+    tells = []
+    for offset in range(1, count):
+        copy = remote(
+            tell_send,
+            tell_recv.at[offset],
+            tell_out.at[offset],
+            tell_in.at[offset],
+            (me, peers[offset]),
+        )
+        copy.start()
+        tells.append(copy)
+    for copy in tells:
+        copy.wait_recv()
+    everything = note
+    for offset in range(1, count):
+        everything = everything + tell_recv[offset]
+    norm = jnp.sqrt(jnp.sum(jnp.where(spot_norm, everything, 0.0), keepdims=True))
+    loss_out[...] = jnp.sum(jnp.where(spot_loss, note, 0.0), keepdims=True)
+    norm_out[...] = norm
+    factor = jnp.minimum(1.0, CLIP_LIMIT / norm)
+    for m in range(8):
+        rotated = turned[m] * factor
+        new_first = BETA_FIRST * first[m] + (1.0 - BETA_FIRST) * rotated
+        new_second = BETA_SECOND * second[m] + (1.0 - BETA_SECOND) * rotated * rotated
+        first_out[m] = new_first
+        second_out[m] = new_second
+        normed = (
+            new_first
+            / (1.0 - BETA_FIRST**ADAM_STEP)
+            / (jnp.sqrt(new_second / (1.0 - BETA_SECOND**ADAM_STEP)) + ADAM_EPS)
+        )
+        back = lax.dot_general(
+            normed,
+            bases[m],
+            (((1,), (1,)), ((), ())),
+            precision=HIGH_PRECISION,
+            preferred_element_type=jnp.float32,
+        )
+        master_out[m] = master[m] - LEARN_RATE * (back + DECAY_RATE * master[m])
+    for copy in started + tells:
+        copy.wait_send()
+
+
+def fold_call(fulls, groups, losses, master, first_moment, second_moment, bases):
+    shards = lax.axis_size("dp")
+    count = lax.axis_size("mp")
+    splits = shards.bit_length() - 1
+    width = fulls[0].shape[1]
+    pile = 4 * (fulls[0].shape[0] + groups[0].shape[0]) // shards
+    own = 4 * fulls[0].shape[0] // (shards * count)
+    low = jnp.bfloat16
+    halves = [shards >> (k + 1) for k in range(splits)]
+    dma = pltpu.SemaphoreType.DMA
+    scratch = (
+        [pltpu.VMEM((half, pile, width), low) for half in halves] * 2
+        + [pltpu.VMEM((half, pile, width), jnp.float32) for half in halves]
+        + [pltpu.VMEM((count, own, width), low)] * 2
+        + [pltpu.VMEM((4 * groups[0].shape[0] // shards, width), low)] * 2
+        + [pltpu.VMEM((splits, 8, 128), jnp.float32)] * 2
+        + [pltpu.VMEM((8, 128), jnp.float32), pltpu.VMEM((count, 8, 128), jnp.float32)]
+        + [dma((splits,))] * 2
+        + [dma((count,))] * 2
+        + [dma(())] * 2
+        + [dma((splits,))] * 2
+        + [dma((count,))] * 2
+    )
+    scalar = jax.ShapeDtypeStruct((1, 1), jnp.float32)
+    state = jax.ShapeDtypeStruct(master.shape, jnp.float32)
+    return line_call(
+        functools.partial(fold_kernel, splits, count),
+        "fold",
+        3,
+        [scalar, scalar, state, state, state],
+        scratch,
+        [*fulls, *groups, losses, master, first_moment, second_moment, bases],
+    )
 
 
 def per_device(
@@ -485,7 +720,7 @@
         (stats[0].reshape(rows), stats[1].reshape(rows), stats[2].reshape(rows)), "mp", merge_stats
     )
     spread_all = top_score + jnp.log(row_total)
-    local_loss = jnp.sum((spread_all - target_logit) * row_weight)
+    losses = ((spread_all - target_logit) * row_weight).reshape(rows // 128, 128)
 
     def block_back(pieces):
         rows_here, target_here, spread_local, weight_here = pieces
@@ -557,27 +792,16 @@
             )
         )
     local_grads.append(grad_out_a)
-    placed = lax.dynamic_update_slice(
-        jnp.zeros((4, D, R), jnp.float32), jnp.stack(local_grads), (0, group_index * group_width, 0)
-    )
-    gradient = jnp.concatenate([jnp.stack(complete_gradients), placed, grad_out_b[None]], 0)
-    owned = lax.psum_scatter(gradient, ("dp", "mp"), scatter_dimension=1, tiled=True)
-    squares = jnp.sum(owned * owned)
-    norm_squared = lax.psum(squares, ("dp", "mp"))
-    mean_loss = lax.psum(local_loss, "dp")
-    grad_norm = jnp.sqrt(norm_squared)
-    clipped = owned * jnp.minimum(1.0, CLIP_LIMIT / grad_norm)
-    rotated = jnp.einsum("mdr,mrs->mds", clipped, eigen_bases, precision=HIGH_PRECISION)
-    new_first = BETA_FIRST * first_moment + (1.0 - BETA_FIRST) * rotated
-    new_second = BETA_SECOND * second_moment + (1.0 - BETA_SECOND) * rotated * rotated
-    normed = (
-        new_first
-        / (1.0 - BETA_FIRST**ADAM_STEP)
-        / (jnp.sqrt(new_second / (1.0 - BETA_SECOND**ADAM_STEP)) + ADAM_EPS)
-    )
-    turned = jnp.einsum("mds,mrs->mdr", normed, eigen_bases, precision=HIGH_PRECISION)
-    new_master = master - LEARN_RATE * (turned + DECAY_RATE * master)
-    return (mean_loss, grad_norm, new_first, new_second, new_master)
+    mean_loss, grad_norm, new_first, new_second, new_master = fold_call(
+        [*complete_gradients, grad_out_b],
+        local_grads,
+        losses,
+        master,
+        first_moment,
+        second_moment,
+        eigen_bases,
+    )
+    return (mean_loss.reshape(()), grad_norm.reshape(()), new_first, new_second, new_master)
 
 
 def solution(mesh):

time: 801 us -> 637 us (0.80)
  waiting for transfers between devices: 149 us -> 0.06 us
  blocking collectives: 90.9 us -> 39.6 us
  Pallas kernels: 187 us -> 223 us
    reduce_scatter x1 -> x0, waiting for transfers between devices: 149 us -> none  [per_device(): lax.psum_scatter(gradient, ('dp', 'mp'), scatter_dimension=1, tiled=True)]
    psum x2 -> x0, blocking collectives: 51.3 us -> none  [the longest x1 38.9 us: per_device(): norm_squared = lax.psum(squares, ('dp', 'mp'))]
    pallas_call x3 -> x4, Pallas kernels: 187 us -> 223 us  [line_call(): pl.pallas_call(kernel, name=name, out_shape=outs, in_specs=[vmem] * len(o...]
  transfers between devices with their start and end apart: 3 -> 2, of which waited for: 1 -> 0; matrix products, arithmetic and copies ran while one was open for 9% -> 11% of each run, Pallas kernels for 17% -> 21%
where the time goes in v2:
time: 637 us; the launch traced here: 632 us
  matrix products  270 us (42%)
  Pallas kernels  223 us (35%)
  other arithmetic  41.7 us (7%)
  blocking collectives  39.6 us (6%)
  local copies, waits for them, and re-layouts  36.1 us (6%)
  between operations  20.7 us (3%)
    pallas_call x4, Pallas kernels, line_call(): pl.pallas_call(kernel, name=name, out_shape=outs, in_specs=[vmem] * len(o...  223 us
    dot_general x4, matrix products, block_back(): jnp.einsum('lv,dv->ld', logit_grad, head_local, preferred_element_type=jn...  132 us
    dot_general x4, matrix products, block_stats(): logits = jnp.dot(rows_here, head_local, preferred_element_type=jnp.float32)  75.4 us
    all_gather x3, blocking collectives, merged(): pieces = jax.tree.map(lambda part: lax.all_gather(part, axis), value)  39.6 us
    reduce_sum x4, other arithmetic, block_stats(): return (top_score, row_total, jnp.sum(jnp.where(hit, logits, 0.0), -1))  26.9 us
    gather x1, local copies, waits for them, and re-layouts, per_device(): embedding[jnp.clip(relative, 0, width - 1)].astype(jnp.float32)  17.7 us
    dot_general x1, matrix products, per_device(): jnp.dot(hidden, w_down, preferred_element_type=jnp.float32)  16.1 us
    unnamed x112, local copies, waits for them, and re-layouts  14.2 us
  transfers between devices with their start and end apart: 2, of which 0 were waited for; matrix products, arithmetic and copies ran while one was open for 11% of the time, Pallas kernels for 21%

profile of v2, /device:TPU:0, one launch (start us, length us, event | category | flops | bytes accessed | tf_op | source)
XLA Modules:
  0.0 631.7 jit_solution(16853032080399929180)
XLA Ops:
  9.0 5.7 copy.47
  19.8 17.7 %gather_fusion = bf16[1024,1024]{1,0:T(8,128)(2,1)} fusion(bf16[12576,1024]{1,0:T(8,128)(2,1)} %param.37, s32[1024]{0:T(1024)S(1)} %broadcast_clamp_fusion), kind=kCustom, calls=%fused_computation | custom fusion | bytes 4198400 | tf_op jit(solution)/shard_map/gather | solution.py:631
  37.7 3.4 select_convert_fusion.part
  41.0 70.4 %start_rows.1 = (bf16[1024,1024]{1,0:T(8,128)(2,1)}, bf16[1024,1024]{1,0:T(8,128)(2,1)}, bf16[1024,1024]{1,0:T(8,128)(2,1)}) custom-call(bf16[1024,1024]{1,0:T(8,128)(2,1)} %select_convert_fusion.part, f32[3,1024]{1,0:T(4,128)} %gain.5, f32[3,1024]{1,0:T(4,128)} %shift.3), custom_call_target="tpu_custom_call" | custom-call | bytes 108413184 | tf_op jit(solution)/shard_map/start_rows/pallas_call | solution.py:306
  112.2 5.6 fusion.155
  117.8 16.1 %fusion.41 = f32[1024,1024]{1,0:T(8,128)} fusion(bf16[1024,1024]{1,0:T(8,128)(2,1)S(1)} %copy-done, f32[1024]{0:T(1024)S(1)} %copy-done.46, bf16[1024,1024]{1,0:T(8,128)(2,1)} %get-tuple-element.331, bf16[1024,1024]{1,0:T(8,128)(2,1)} %param.40), kind=kOutput, calls=%fused_computation.73 | convolution fusion | flops 4364173312 | bytes 10489856 | tf_op jit(solution)/shard_map/dot_general | solution.py:694
  135.5 3.0 convolution_convert_fusion
  146.8 2.1 fusion.68
  151.7 3.0 add_convert_fusion.part
  154.6 61.1 %resid_rows.1 = (f32[1024,1024]{1,0:T(8,128)}, bf16[1024,1024]{1,0:T(8,128)(2,1)}) custom-call(bf16[1024,1024]{1,0:T(8,128)(2,1)} %add_convert_fusion.part, bf16[1024,1024]{1,0:T(8,128)(2,1)} %get-tuple-element.332.start, f32[3,1024]{1,0:T(4,128)} %gain.5, f32[3,1024]{1,0:T(4,128)} %shift.3), custom_call_target="tpu_custom_call" | custom-call | bytes 110510336 | tf_op jit(solution)/shard_map/resid_rows/pallas_call | solution.py:306
  217.0 102.9 %while.54 = (s32[]{:T(128)}, f32[4,256]{1,0:T(4,128)S(1)}, f32[4,256]{1,0:T(4,128)S(1)}, f32[4,256]{1,0:T(4,128)S(1)}, bf16[4,256,1024]{2,1,0:T(8,128)(2,1)}, /*...) while((s32[]{:T(128)}, f32[4,256]{1,0:T(4,128)S(1)}, ...), condition=%wide.region_8.9_spmd.clone.clone, body=%wide.region_4.8_spmd.clone.sunk.clone | while | flops 6612762112 | bytes 52246120 | solution.py:716
  217.0 18.9 %fusion.219 = (f32[256]{0:T(256)S(1)}, f32[256,12576]{0,1:T(8,128)}) fusion(bf16[1024,12576]{1,0:T(8,128)(2,1)} %get-tuple-element.719, bf16[4,256,1024]{2,1,0:T(8,128)(2,1)} %get-tuple-element.718, s32[]{:T(128)} %get-tuple-element.706), kind=kOutput, calls=%fused_computation.236.clone.1.clone | convolution fusion | flops 6596665344 | bytes 39355904 | tf_op jit(solution)/shard_map/while/body/eval_jaxpr/dot_general | solution.py:710
  235.9 6.7 %select_reduce_fusion.3 = (f32[256]{0:T(256)S(1)}, f32[256]{0:T(256)S(1)}) fusion(f32[256,12576]{0,1:T(8,128)} %get-tuple-element.665, s32[256]{0:T(256)S(1)} %bitcast.295, f32[256]{0:T(256)S(1)} %get-tuple-element.664), kind=kLoop, calls=%fused_computation.8.clone.1.clone | loop fusion | flops 16096768 | bytes 12881920 | tf_op jit(solution)/shard_map/while/body/eval_jaxpr/reduce_sum | solution.py:714
  242.7 18.9 %fusion.219 = (f32[256]{0:T(256)S(1)}, f32[256,12576]{0,1:T(8,128)}) fusion(bf16[1024,12576]{1,0:T(8,128)(2,1)} %get-tuple-element.719, bf16[4,256,1024]{2,1,0:T(8,128)(2,1)} %get-tuple-element.718, s32[]{:T(128)} %get-tuple-element.706), kind=kOutput, calls=%fused_computation.236.clone.1.clone | convolution fusion | flops 6596665344 | bytes 39355904 | tf_op jit(solution)/shard_map/while/body/eval_jaxpr/dot_general | solution.py:710
  261.6 6.7 %select_reduce_fusion.3 = (f32[256]{0:T(256)S(1)}, f32[256]{0:T(256)S(1)}) fusion(f32[256,12576]{0,1:T(8,128)} %get-tuple-element.665, s32[256]{0:T(256)S(1)} %bitcast.295, f32[256]{0:T(256)S(1)} %get-tuple-element.664), kind=kLoop, calls=%fused_computation.8.clone.1.clone | loop fusion | flops 16096768 | bytes 12881920 | tf_op jit(solution)/shard_map/while/body/eval_jaxpr/reduce_sum | solution.py:714
  268.5 18.9 %fusion.219 = (f32[256]{0:T(256)S(1)}, f32[256,12576]{0,1:T(8,128)}) fusion(bf16[1024,12576]{1,0:T(8,128)(2,1)} %get-tuple-element.719, bf16[4,256,1024]{2,1,0:T(8,128)(2,1)} %get-tuple-element.718, s32[]{:T(128)} %get-tuple-element.706), kind=kOutput, calls=%fused_computation.236.clone.1.clone | convolution fusion | flops 6596665344 | bytes 39355904 | tf_op jit(solution)/shard_map/while/body/eval_jaxpr/dot_general | solution.py:710
  287.3 6.7 %select_reduce_fusion.3 = (f32[256]{0:T(256)S(1)}, f32[256]{0:T(256)S(1)}) fusion(f32[256,12576]{0,1:T(8,128)} %get-tuple-element.665, s32[256]{0:T(256)S(1)} %bitcast.295, f32[256]{0:T(256)S(1)} %get-tuple-element.664), kind=kLoop, calls=%fused_computation.8.clone.1.clone | loop fusion | flops 16096768 | bytes 12881920 | tf_op jit(solution)/shard_map/while/body/eval_jaxpr/reduce_sum | solution.py:714
  294.2 18.8 %fusion.219 = (f32[256]{0:T(256)S(1)}, f32[256,12576]{0,1:T(8,128)}) fusion(bf16[1024,12576]{1,0:T(8,128)(2,1)} %get-tuple-element.719, bf16[4,256,1024]{2,1,0:T(8,128)(2,1)} %get-tuple-element.718, s32[]{:T(128)} %get-tuple-element.706), kind=kOutput, calls=%fused_computation.236.clone.1.clone | convolution fusion | flops 6596665344 | bytes 39355904 | tf_op jit(solution)/shard_map/while/body/eval_jaxpr/dot_general | solution.py:710
  313.0 6.7 %select_reduce_fusion.3 = (f32[256]{0:T(256)S(1)}, f32[256]{0:T(256)S(1)}) fusion(f32[256,12576]{0,1:T(8,128)} %get-tuple-element.665, s32[256]{0:T(256)S(1)} %bitcast.295, f32[256]{0:T(256)S(1)} %get-tuple-element.664), kind=kLoop, calls=%fused_computation.8.clone.1.clone | loop fusion | flops 16096768 | bytes 12881920 | tf_op jit(solution)/shard_map/while/body/eval_jaxpr/reduce_sum | solution.py:714
  319.9 13.2 %all-gather = f32[4,1,1024]{2,1,0:T(1,128)S(1)} all-gather(f32[1,1,1024]{2,1,0:T(1,128)S(1)} %reshape.521), channel_id=1, replica_groups=mesh['dp'=8,'mp'=4] {'mp'}, dimensions={0}, use_global_device_ids=true | all-gather | bytes 20480 | tf_op jit(solution)/shard_map/all_gather | solution.py:33
  333.1 13.2 %all-gather.1 = f32[4,1,1024]{2,1,0:T(1,128)S(1)} all-gather(f32[1,1,1024]{2,1,0:T(1,128)S(1)} %reshape.523), channel_id=1, replica_groups=mesh['dp'=8,'mp'=4] {'mp'}, dimensions={0}, use_global_device_ids=true | all-gather | bytes 20480 | tf_op jit(solution)/shard_map/all_gather | solution.py:33
  346.3 13.2 %all-gather.2 = f32[4,1,1024]{2,1,0:T(1,128)S(1)} all-gather(f32[1,1,1024]{2,1,0:T(1,128)S(1)} %reshape.525), channel_id=1, replica_groups=mesh['dp'=8,'mp'=4] {'mp'}, dimensions={0}, use_global_device_ids=true | all-gather | bytes 20480 | tf_op jit(solution)/shard_map/all_gather | solution.py:33
  360.5 132.5 %while.55 = (s32[]{:T(128)}, bf16[4,256,1024]{2,1,0:T(8,128)(2,1)S(1)}, bf16[4,256,1024]{2,1,0:T(8,128)(2,1)}, bf16[1024,12576]{1,0:T(8,128)(2,1)}, f32[4,256]{1...) while((s32[]{:T(128)}, ...), condition=%wide.region_13.14_spmd.clone.clone, body=%wide.region_12.13_spmd.clone.sunk.clone | while | flops 13206208512 | bytes 53487712 | solution.py:734
  360.5 33.1 %fusion.224 = bf16[4,256,1024]{2,1,0:T(8,128)(2,1)S(1)} fusion(bf16[4,256,1024]{2,1,0:T(8,128)(2,1)S(1)} %get-tuple-element.752, s32[]{:T(128)} %get-tuple-element.751, bf16[1024,12576]{1,0:T(8,128)(2,1)} %get-tuple-element.762, f32[256]{0:T(256)S(1)} %bitcast.300, s32[256]{0:T(256)S(1)} %bitcast.299, f32[256]{0:T(256)S(1)} %bitcast.301, ...), kind=kOutput, calls=%fused_computation.22.clone.1.clone | convolution fusion | flops 13206208512 | bytes 53481472 | tf_op jit(solution)/shard_map/while/body/eval_jaxpr/lv,dv->ld/dot_general | solution.py:732
  393.6 33.1 %fusion.224 = bf16[4,256,1024]{2,1,0:T(8,128)(2,1)S(1)} fusion(bf16[4,256,1024]{2,1,0:T(8,128)(2,1)S(1)} %get-tuple-element.752, s32[]{:T(128)} %get-tuple-element.751, bf16[1024,12576]{1,0:T(8,128)(2,1)} %get-tuple-element.762, f32[256]{0:T(256)S(1)} %bitcast.300, s32[256]{0:T(256)S(1)} %bitcast.299, f32[256]{0:T(256)S(1)} %bitcast.301, ...), kind=kOutput, calls=%fused_computation.22.clone.1.clone | convolution fusion | flops 13206208512 | bytes 53481472 | tf_op jit(solution)/shard_map/while/body/eval_jaxpr/lv,dv->ld/dot_general | solution.py:732
  426.8 33.1 %fusion.224 = bf16[4,256,1024]{2,1,0:T(8,128)(2,1)S(1)} fusion(bf16[4,256,1024]{2,1,0:T(8,128)(2,1)S(1)} %get-tuple-element.752, s32[]{:T(128)} %get-tuple-element.751, bf16[1024,12576]{1,0:T(8,128)(2,1)} %get-tuple-element.762, f32[256]{0:T(256)S(1)} %bitcast.300, s32[256]{0:T(256)S(1)} %bitcast.299, f32[256]{0:T(256)S(1)} %bitcast.301, ...), kind=kOutput, calls=%fused_computation.22.clone.1.clone | convolution fusion | flops 13206208512 | bytes 53481472 | tf_op jit(solution)/shard_map/while/body/eval_jaxpr/lv,dv->ld/dot_general | solution.py:732
  459.9 33.0 %fusion.224 = bf16[4,256,1024]{2,1,0:T(8,128)(2,1)S(1)} fusion(bf16[4,256,1024]{2,1,0:T(8,128)(2,1)S(1)} %get-tuple-element.752, s32[]{:T(128)} %get-tuple-element.751, bf16[1024,12576]{1,0:T(8,128)(2,1)} %get-tuple-element.762, f32[256]{0:T(256)S(1)} %bitcast.300, s32[256]{0:T(256)S(1)} %bitcast.299, f32[256]{0:T(256)S(1)} %bitcast.301, ...), kind=kOutput, calls=%fused_computation.22.clone.1.clone | convolution fusion | flops 13206208512 | bytes 53481472 | tf_op jit(solution)/shard_map/while/body/eval_jaxpr/lv,dv->ld/dot_general | solution.py:732
  492.9 55.3 %branch_rows.1 = bf16[1024,1024]{1,0:T(8,128)(2,1)} custom-call(bf16[1024,1024]{1,0:T(8,128)(2,1)S(1)} %bitcast.272, f32[1024,1024]{1,0:T(8,128)} %get-tuple-element.340.resid, f32[3,1024]{1,0:T(4,128)} %gain.5), custom_call_target="tpu_custom_call" | custom-call | bytes 108400896 | tf_op jit(solution)/shard_map/branch_rows/pallas_call | solution.py:306
  548.3 2.5 fusion.156
  560.4 2.6 multiply_reduce_fusion
  568.8 1.9 fusion.56
  580.2 36.3 %fold.1 = (f32[1,1]{1,0:T(1,128)}, f32[1,1]{1,0:T(1,128)}, f32[8,32,128]{2,1,0:T(8,128)}, f32[8,32,128]{2,1,0:T(8,128)}, f32[8,32,128]{2,1,0:T(8,128)}) custom-call(f32[1024,128]{1,0:T(8,128)} %fusion.97.refs_0_, f32[1024,128]{1,0:T(8,128)} %fusion.95.refs_1_, f32[1024,128]{1,0:T(8,128)} %fusion.93.refs_2_, f32[1024,128]{1,0:T(8,128)} %fusion.160.refs_3_, ...), custom_call_target="tpu_custom_call" | custom-call | bytes 103936264 | tf_op jit(solution)/shard_map/fold/pallas_call | solution.py:306
  (231 shorter events, 50.1 us)
Async XLA Ops:
  7.2 110.6 %copy-start = (bf16[1024,1024]{1,0:T(8,128)(2,1)S(1)}, bf16[1024,1024]{1,0:T(8,128)(2,1)}, u32[]{:S(2)}) copy-start(bf16[1024,1024]{1,0:T(8,128)(2,1)} %param.42) | copy-start | bytes 6291460
  7.2 126.7 %all-gather.6.cloned.1.call-start = ((), (), s32[]{:S(2)}) async-start(), calls=%async_computation | async-start | bytes 2162688 | tf_op jit(solution)/shard_map/all_gather | solution.py:619
  8.9 5.8 copy-start.45
  8.9 7.1 %copy-start.48 = (s32[8]{0:T(128)S(1)}, s32[8]{0:T(128)}, u32[]{:S(2)}) copy-start(s32[8]{0:T(128)} %param.35) | copy-start | bytes 100
  9.0 7.7 %copy-start.47 = (s32[8]{0:T(128)S(1)}, s32[8]{0:T(128)}, u32[]{:S(2)}) copy-start(s32[8]{0:T(128)} %param.36) | copy-start | bytes 100
  9.0 208.0 %all-gather.8.cloned.1.call-start = ((), (), s32[]{:S(2)}) async-start(), calls=%async_computation.1 | async-start | bytes 29196288 | tf_op jit(solution)/shard_map/all_gather | solution.py:620
  111.8 27.7 %copy-start.35 = (f32[1024,8]{0,1:T(8,128)}, f32[1024,8]{0,1:T(8,128)S(1)}, u32[]{:S(2)}) copy-start(f32[1024,8]{0,1:T(8,128)S(1)} %get-tuple-element.462) | copy-start | bytes 98308
  111.8 27.7 %copy-start.37 = (f32[1024,8]{0,1:T(8,128)}, f32[1024,8]{0,1:T(8,128)S(1)}, u32[]{:S(2)}) copy-start(f32[1024,8]{0,1:T(8,128)S(1)} %get-tuple-element.463) | copy-start | bytes 98308
  112.2 5.6 copy-start.46
  135.4 13.5 %copy-start.34 = (bf16[1,1024,128]{2,1,0:T(8,128)(2,1)}, bf16[1,1024,128]{2,1,0:T(8,128)(2,1)S(1)}, u32[]{:S(2)}) copy-start(bf16[1,1024,128]{2,1,0:T(8,128)(2,1)S(1)} %get-tuple-element.441) | copy-start | bytes 786436
  135.4 3.1 copy-start.10
  135.5 3.4 copy-start.30
  135.5 4.3 copy-start.32
  140.1 6.1 copy-start.8
  141.1 4.3 copy-start.3
  143.5 3.3 copy-start.2
  146.8 2.5 copy-start.39
  146.8 2.5 copy-start.15
  217.0 143.5 %copy-start.17 = (bf16[4,256,1024]{2,1,0:T(8,128)(2,1)S(1)}, bf16[4,256,1024]{2,1,0:T(8,128)(2,1)}, u32[]{:S(2)}) copy-start(bf16[4,256,1024]{2,1,0:T(8,128)(2,1)} %custom-call.2) | copy-start | bytes 6291460
  492.9 55.3 %copy-start.16 = (bf16[256,1024]{1,0:T(8,128)(2,1)S(1)}, bf16[256,1024]{1,0:T(8,128)(2,1)}, u32[]{:S(2)}) copy-start(bf16[256,1024]{1,0:T(8,128)(2,1)} %param.39) | copy-start | bytes 1572868
  548.2 2.5 copy-start.6
  548.3 4.3 copy-start.40
  548.3 4.3 copy-start.42
  550.8 4.0 copy-start.4
  550.8 4.0 copy-start.44
  556.6 2.6 slice-start
  556.6 3.7 slice-start.1
  557.9 2.5 copy-start.43
  568.8 2.8 copy-start.5
  574.1 3.2 copy-start.29
  575.1 3.6 copy-start.31
  575.9 46.5 %copy-start.1 = (bf16[1024,1024]{1,0:T(8,128)(2,1)S(1)}, bf16[1024,1024]{1,0:T(8,128)(2,1)}, u32[]{:S(2)}) copy-start(bf16[1024,1024]{1,0:T(8,128)(2,1)} %param.42) | copy-start | bytes 6291460
  (21 other events, 33.7 us)
Sparse Core Ops, SparseCore 0:
  11.5 62.7 all-gather.5
  76.1 127.2 all-gather.7

commit v3 on v2

--- a/solution.py
+++ b/solution.py
@@ -27,14 +27,6 @@
 BETA_SECOND = 0.999
 ADAM_EPS = 1e-08
 DECAY_RATE = 0.01
-
-
-def merged(value, axis, join):
-    pieces = jax.tree.map(lambda part: lax.all_gather(part, axis), value)
-    head = jax.tree.map(lambda part: part[0], pieces)
-    tail = jax.tree.map(lambda part: part[1:], pieces)
-    running, _ = lax.scan(lambda running, section: (join(running, section), None), head, tail)
-    return running
 
 
 def layer_norm(values, gain, shift):
@@ -144,14 +136,6 @@
     return (jnp.concatenate(query_grads, 0), key_grad, value_grad)
 
 
-def merge_stats(first, second):
-    top_score = jnp.maximum(first[0], second[0])
-    row_total = first[1] * jnp.exp(first[0] - top_score) + second[1] * jnp.exp(
-        second[0] - top_score
-    )
-    return (top_score, row_total, first[2] + second[2])
-
-
 def line_chunk(index, size):
     return pl.ds(pl.multiple_of(index * size, size), size)
 
@@ -175,7 +159,16 @@
     pl.semaphore_wait(barrier, peers)
 
 
-def line_sum(count, chunk, own, wires, sems, prepare, emit):
+def greet_peers(me, count):
+    barrier = pltpu.get_barrier_semaphore()
+    for offset in range(1, count):
+        pl.semaphore_signal(
+            barrier, inc=1, device_id={"mp": lax.rem(me + offset, count)}, device_id_type=MESH
+        )
+    pl.semaphore_wait(barrier, count - 1)
+
+
+def line_sum(count, chunk, own, wires, sems, prepare, emit, greet=True):
     me = lax.axis_index("mp")
     from_low, from_high, to_high, to_low = wires
     up_send, up_recv, down_send, down_recv = sems
@@ -206,7 +199,8 @@
             device_id_type=MESH,
         )
 
-    greet_line(me, count)
+    if greet:
+        greet_line(me, count)
 
     @pl.when(me == 0)
     def _():
@@ -341,7 +335,45 @@
     line_sum(count, LINE_CHUNK, part, scratch[:4], scratch[4:], None, emit)
 
 
-def branch_kernel(count, part, resid, gain, out, *scratch):
+def branch_kernel(count, raw, hits, stats, weight, resid, gain, out, loss_out, *scratch):
+    own, note_send, note_recv, scales, note_out, note_in = scratch[8:]
+    me = lax.axis_index("mp")
+    rows_all = raw.shape[0]
+    greet_peers(me, count)
+    note_send[...] = stats[...].T[0:8, :]
+    copies = []
+    for offset in range(1, count):
+        copy = pltpu.make_async_remote_copy(
+            src_ref=note_send,
+            dst_ref=note_recv.at[offset],
+            send_sem=note_out.at[offset],
+            recv_sem=note_in.at[offset],
+            device_id={"mp": lax.rem(me + offset, count)},
+            device_id_type=MESH,
+        )
+        copy.start()
+        copies.append(copy)
+    mine = note_send[...]
+    for copy in copies:
+        copy.wait_recv()
+    others = [mine] + [note_recv[offset] for offset in range(1, count)]
+    top = functools.reduce(jnp.maximum, [part[0:1, :] for part in others])
+    total = sum(part[1:2, :] * jnp.exp(part[0:1, :] - top) for part in others)
+    found = sum(part[2:3, :] for part in others)
+    spread_row = top + jnp.log(total)
+    share = weight[...]
+    loss_out[...] = (spread_row - found) * share
+    factor = jnp.exp(mine[0:1, :] - spread_row) * share
+    pair = jnp.concatenate([factor, share, jnp.zeros((126, rows_all), jnp.float32)], 0)
+    scales[...] = pair.T
+
+    def prepare(at):
+        rows = line_chunk(at, LINE_CHUNK)
+        scale = scales[rows, :]
+        own[rows, :] = (
+            raw[rows, :] * scale[:, 0:1] - hits[rows, :].astype(jnp.float32) * scale[:, 1:2]
+        ).astype(jnp.bfloat16)
+
     def emit(rows, total):
         values = resid[rows, :]
         centre = values - jnp.mean(values, -1, keepdims=True)
@@ -358,7 +390,97 @@
             )
         ).astype(jnp.bfloat16)
 
-    line_sum(count, LINE_CHUNK, part, scratch[:4], scratch[4:], None, emit)
+    line_sum(count, LINE_CHUNK, own, scratch[:4], scratch[4:8], prepare, emit, greet=False)
+    for copy in copies:
+        copy.wait_send()
+
+
+def loss_kernel(vocab, tile, values, ahead, behind, hits, acc, stats, logits, probs, tops, sums):
+    at = pl.program_id(0)
+    tiles = pl.num_programs(0) - 1
+    rows_all = values.shape[0]
+
+    @pl.when(at == 0)
+    def _():
+        acc[...] = jnp.zeros_like(acc)
+        tops[...] = jnp.full_like(tops, -1e29)
+        sums[...] = jnp.zeros_like(sums)
+        logits[...] = jnp.full_like(logits, -1e30)
+
+    tail = vocab % tile
+    if tail:
+
+        @pl.when(at >= tiles - 1)
+        def _():
+            ahead[tail:, :] = jnp.zeros((tile - tail, ahead.shape[1]), ahead.dtype)
+
+        @pl.when(at >= tiles)
+        def _():
+            behind[tail:, :] = jnp.zeros((tile - tail, behind.shape[1]), behind.dtype)
+
+    ids = (at - 1) * tile + lax.broadcasted_iota(jnp.int32, (1, tile), 1)
+    scores = logits[...] + jnp.where(ids < vocab, 0.0, -1e30)
+    old = tops[:, 0:1]
+    new = jnp.maximum(old, jnp.max(scores, -1, keepdims=True))
+    weights = jnp.exp(scores - new)
+    shrink = jnp.exp(old - new)
+    sums[...] = sums[...] * shrink + jnp.sum(weights, -1, keepdims=True)
+    tops[...] = jnp.broadcast_to(new, tops.shape)
+    acc[...] = acc[...] * shrink
+    probs[...] = weights.astype(jnp.bfloat16)
+    logits[...] = lax.dot_general(
+        values[...], ahead[...], (((1,), (1,)), ((), ())), preferred_element_type=jnp.float32
+    )
+    acc[...] += jnp.dot(probs[...], behind[...], preferred_element_type=jnp.float32)
+
+    @pl.when(at == tiles)
+    def _():
+        found = jnp.sum(
+            values[...].astype(jnp.float32) * hits[...].astype(jnp.float32), -1, keepdims=True
+        )
+        column = lax.broadcasted_iota(jnp.int32, (rows_all, 128), 1)
+        stats[...] = jnp.where(
+            column == 0, tops[...], jnp.where(column == 1, sums[...], found)
+        )
+
+
+LOSS_TILE = 512
+
+
+def loss_call(values, head_rows, hits):
+    rows, width = values.shape
+    vocab = head_rows.shape[0]
+    tile = LOSS_TILE
+    tiles = pl.cdiv(vocab, tile)
+    whole = pl.BlockSpec((rows, width), lambda j: (0, 0))
+    return pl.pallas_call(
+        functools.partial(loss_kernel, vocab, tile),
+        name="loss",
+        grid=(tiles + 1,),
+        in_specs=[
+            whole,
+            pl.BlockSpec((tile, width), lambda j: (jnp.minimum(j, tiles - 1), 0)),
+            pl.BlockSpec((tile, width), lambda j: (jnp.maximum(j - 1, 0), 0)),
+            whole,
+        ],
+        out_specs=[whole, pl.BlockSpec((rows, 128), lambda j: (0, 0))],
+        out_shape=[
+            jax.ShapeDtypeStruct((rows, width), jnp.float32),
+            jax.ShapeDtypeStruct((rows, 128), jnp.float32),
+        ],
+        scratch_shapes=[
+            pltpu.VMEM((rows, tile), jnp.float32),
+            pltpu.VMEM((rows, tile), jnp.bfloat16),
+            pltpu.VMEM((rows, 128), jnp.float32),
+            pltpu.VMEM((rows, 128), jnp.float32),
+        ],
+        compiler_params=pltpu.CompilerParams(vmem_limit_bytes=VMEM_LIMIT),
+        cost_estimate=pl.CostEstimate(
+            flops=4 * rows * width * vocab,
+            bytes_accessed=4 * width * vocab,
+            transcendentals=rows * vocab,
+        ),
+    )(values, head_rows, head_rows, hits)
 
 
 def fold_kernel(splits, count, *refs):
@@ -617,10 +739,10 @@
     group_count = lax.axis_size("mp")
     group_index = lax.axis_index("mp")
     adapters = lax.all_gather(master.astype(jnp.bfloat16), ("dp", "mp"), axis=1, tiled=True)
-    head_local = lax.all_gather(unembed, "dp", axis=0, tiled=True)
+    head_rows = lax.all_gather(unembed.T, "dp", axis=1, tiled=True)
     examples, length = token_ids.shape
     width = embedding.shape[0]
-    vocab_local = head_local.shape[1]
+    vocab_local = head_rows.shape[0]
     rows = examples * length
     local_heads = HEADS // group_count
     group_width = local_heads * HD
@@ -701,52 +823,27 @@
         line_scratch(rows, D),
         [partial_value.astype(jnp.bfloat16), start_rows, ln_gain, ln_bias],
     )
-    row_block = min(256, rows)
-    blocks = rows // row_block
-    vocab_ids = jnp.arange(vocab_local)[None, :]
-
-    def block_stats(pieces):
-        rows_here, target_here = pieces
-        logits = jnp.dot(rows_here, head_local, preferred_element_type=jnp.float32)
-        top_score = jnp.max(logits, -1)
-        row_total = jnp.sum(jnp.exp(logits - top_score[:, None]), -1)
-        hit = vocab_ids == (target_here - group_index * vocab_local)[:, None]
-        return (top_score, row_total, jnp.sum(jnp.where(hit, logits, 0.0), -1))
-
-    stats = lax.map(
-        block_stats, (final_rows.reshape(blocks, row_block, D), target.reshape(blocks, row_block))
-    )
-    top_score, row_total, target_logit = merged(
-        (stats[0].reshape(rows), stats[1].reshape(rows), stats[2].reshape(rows)), "mp", merge_stats
-    )
-    spread_all = top_score + jnp.log(row_total)
-    losses = ((spread_all - target_logit) * row_weight).reshape(rows // 128, 128)
-
-    def block_back(pieces):
-        rows_here, target_here, spread_local, weight_here = pieces
-        logits = jnp.dot(rows_here, head_local, preferred_element_type=jnp.float32)
-        hit = (vocab_ids == (target_here - group_index * vocab_local)[:, None]).astype(jnp.float32)
-        logit_grad = (
-            (jnp.exp(logits - spread_local[:, None]) - hit) * weight_here[:, None]
-        ).astype(jnp.bfloat16)
-        return jnp.einsum("lv,dv->ld", logit_grad, head_local, preferred_element_type=jnp.float32)
-
-    head_grad = lax.map(
-        block_back,
-        (
-            final_rows.reshape(blocks, row_block, D),
-            target.reshape(blocks, row_block),
-            spread_all.reshape(blocks, row_block),
-            row_weight.reshape(blocks, row_block),
-        ),
-    ).reshape(rows, D)
-    (branch_grad,) = line_call(
+    goal = target - group_index * vocab_local
+    near = (goal >= 0) & (goal < vocab_local)
+    hits = jnp.where(near[:, None], head_rows[jnp.clip(goal, 0, vocab_local - 1)], 0.0).astype(
+        jnp.bfloat16
+    )
+    raw_grad, stats = loss_call(final_rows, head_rows, hits)
+    branch_grad, losses = line_call(
         functools.partial(branch_kernel, group_count),
         "branch_rows",
         2,
-        [shape_low],
-        line_scratch(rows, D),
-        [head_grad.astype(jnp.bfloat16), resid, ln_gain],
+        [shape_low, jax.ShapeDtypeStruct((1, rows), jnp.float32)],
+        line_scratch(rows, D)
+        + [
+            pltpu.VMEM((rows, D), jnp.bfloat16),
+            pltpu.VMEM((8, rows), jnp.float32),
+            pltpu.VMEM((group_count, 8, rows), jnp.float32),
+            pltpu.VMEM((rows, 128), jnp.float32),
+            pltpu.SemaphoreType.DMA((group_count,)),
+            pltpu.SemaphoreType.DMA((group_count,)),
+        ],
+        [raw_grad, hits, stats, row_weight.reshape(1, rows), resid, ln_gain],
     )
     inner_out_grad = jnp.dot(branch_grad, adapters[7], preferred_element_type=jnp.float32).astype(
         jnp.bfloat16

time: 637 us -> 464 us (0.73)
  matrix products: 270 us -> 64.2 us
  Pallas kernels: 223 us -> 305 us
  blocking collectives: 39.6 us -> 0 us
  other arithmetic: 41.7 us -> 19.6 us
  local copies, waits for them, and re-layouts: 36.1 us -> 48.7 us
    dot_general x8 -> x0, matrix products: 208 us -> none  [the longest x4 132 us: block_back(): jnp.einsum('lv,dv->ld', logit_grad, head_local, preferred_element_type=jn...]
    pallas_call x0 -> x1, Pallas kernels: none -> 71.4 us  [loss_call(): pl.pallas_call(functools.partial(loss_kernel, vocab, tile), name='loss',...]
    all_gather x3 -> x0, blocking collectives: 39.6 us -> none  [merged(): pieces = jax.tree.map(lambda part: lax.all_gather(part, axis), value)]
    reduce_sum x4 -> x0, other arithmetic: 26.9 us -> none  [block_stats(): return (top_score, row_total, jnp.sum(jnp.where(hit, logits, 0.0), -1))]
    gather x0 -> x1, local copies, waits for them, and re-layouts: none -> 17 us  [per_device(): head_rows[jnp.clip(goal, 0, vocab_local - 1)]]
    pallas_call x4, Pallas kernels: 223 us -> 234 us  [line_call(): pl.pallas_call(kernel, name=name, out_shape=outs, in_specs=[vmem] * len(o...]
    unnamed x112 -> x87, local copies, waits for them, and re-layouts: 14.2 us -> 7.68 us
  transfers between devices with their start and end apart: 2 -> 2, of which waited for: 0 -> 0; matrix products, arithmetic and copies ran while one was open for 11% -> 16% of each run, Pallas kernels for 21% -> 29%
where the time goes in v3:
time: 464 us; the launch traced here: 459 us
  Pallas kernels  305 us (66%)
  matrix products  64.2 us (14%)
  local copies, waits for them, and re-layouts  48.7 us (10%)
  between operations  20.7 us (4%)
  other arithmetic  19.6 us (4%)
    pallas_call x4, Pallas kernels, line_call(): pl.pallas_call(kernel, name=name, out_shape=outs, in_specs=[vmem] * len(o...  234 us
    pallas_call x1, Pallas kernels, loss_call(): pl.pallas_call(functools.partial(loss_kernel, vocab, tile), name='loss',...  71.4 us
    gather x1, local copies, waits for them, and re-layouts, per_device(): embedding[jnp.clip(relative, 0, width - 1)].astype(jnp.float32)  17.7 us
    gather x1, local copies, waits for them, and re-layouts, per_device(): head_rows[jnp.clip(goal, 0, vocab_local - 1)]  17 us
    dot_general x1, matrix products, per_device(): jnp.dot(hidden, w_down, preferred_element_type=jnp.float32)  16.1 us
  transfers between devices with their start and end apart: 2, of which 0 were waited for; matrix products, arithmetic and copies ran while one was open for 16% of the time, Pallas kernels for 29%

profile of v3, /device:TPU:0, one launch (start us, length us, event | category | flops | bytes accessed | tf_op | source)
XLA Modules:
  0.0 459.0 jit_solution(10753908303829482720)
XLA Ops:
  7.2 1.7 convert_element_type.98
  18.1 17.7 %gather_fusion = bf16[1024,1024]{1,0:T(8,128)(2,1)} fusion(bf16[12576,1024]{1,0:T(8,128)(2,1)} %param.31, s32[1024]{0:T(1024)S(1)} %broadcast_clamp_fusion.1), kind=kCustom, calls=%fused_computation | custom fusion | bytes 4198400 | tf_op jit(solution)/shard_map/gather | solution.py:753
  35.9 3.3 select_convert_fusion.part
  39.2 70.7 %start_rows.1 = (bf16[1024,1024]{1,0:T(8,128)(2,1)}, bf16[1024,1024]{1,0:T(8,128)(2,1)}, bf16[1024,1024]{1,0:T(8,128)(2,1)}) custom-call(bf16[1024,1024]{1,0:T(8,128)(2,1)} %select_convert_fusion.part, f32[3,1024]{1,0:T(4,128)} %gain.5, f32[3,1024]{1,0:T(4,128)} %shift.3), custom_call_target="tpu_custom_call" | custom-call | bytes 108413184 | tf_op jit(solution)/shard_map/start_rows/pallas_call | solution.py:300
  114.6 5.5 %fusion.129 = f32[1024,768]{0,1:T(8,128)} fusion(bf16[1024,1024]{1,0:T(8,128)(2,1)} %get-tuple-element.83, bf16[1024,768]{1,0:T(8,128)(2,1)} %param.32), kind=kOutput, calls=%fused_computation.205 | convolution fusion | flops 1610612736 | bytes 6815744 | tf_op jit(solution)/shard_map/dot_general | solution.py:778
  120.2 16.1 %fusion.21 = f32[1024,1024]{1,0:T(8,128)} fusion(bf16[1024,1024]{1,0:T(8,128)(2,1)S(1)} %copy-done, f32[1024]{0:T(1024)S(1)} %copy-done.39, bf16[1024,1024]{1,0:T(8,128)(2,1)} %get-tuple-element.84, bf16[1024,1024]{1,0:T(8,128)(2,1)} %param.34), kind=kOutput, calls=%fused_computation.45 | convolution fusion | flops 4364173312 | bytes 10489856 | tf_op jit(solution)/shard_map/dot_general | solution.py:816
  136.3 1.6 fusion.125
  138.0 3.1 convolution_convert_fusion
  144.2 1.8 fusion.127
  146.0 1.9 fusion
  149.2 2.1 fusion.48
  152.5 1.5 copy-done.7
  154.0 3.0 add_convert_fusion.part
  157.1 60.7 %resid_rows.1 = (f32[1024,1024]{1,0:T(8,128)}, bf16[1024,1024]{1,0:T(8,128)(2,1)}) custom-call(bf16[1024,1024]{1,0:T(8,128)(2,1)} %add_convert_fusion.part, bf16[1024,1024]{1,0:T(8,128)(2,1)} %get-tuple-element.85.start, f32[3,1024]{1,0:T(4,128)} %gain.5, f32[3,1024]{1,0:T(4,128)} %shift.3), custom_call_target="tpu_custom_call" | custom-call | bytes 110510336 | tf_op jit(solution)/shard_map/resid_rows/pallas_call | solution.py:300
  217.8 17.0 %gather_fusion.1 = bf16[1024,1024]{1,0:T(8,128)(2,1)S(1)} fusion(bf16[12576,1024]{1,0:T(8,128)(2,1)} %all-gather.5.cloned.1.call-done.ahead.behind, s32[1024]{0:T(1024)} %broadcast_clamp_fusion), kind=kCustom, calls=%fused_computation.1 | custom fusion | bytes 4198400 | tf_op jit(solution)/shard_map/gather | solution.py:828
  234.8 2.2 broadcast_select_fusion.hits
  237.0 71.4 %loss.1 = (f32[1024,1024]{1,0:T(8,128)}, f32[1024,128]{1,0:T(8,128)}) custom-call(bf16[1024,1024]{1,0:T(8,128)(2,1)} %get-tuple-element.86.values, bf16[12576,1024]{1,0:T(8,128)(2,1)} %all-gather.5.cloned.1.call-done.ahead.behind, bf16[12576,1024]{1,0:T(8,128)(2,1)} %all-gather.5.cloned.1.call-done.ahead.behind, bf16[1024,1024]{1,0:T(8,128)(2,1)} %broadcast_select_fusion.hits), custom_call_target="tpu_custom_call" | custom-call | flops 52747567104 | bytes 51511296 | tf_op jit(solution)/shard_map/loss/pallas_call | solution.py:456
  308.5 65.5 %branch_rows.1 = (bf16[1024,1024]{1,0:T(8,128)(2,1)}, f32[1,1024]{1,0:T(1,128)}) custom-call(f32[1024,1024]{1,0:T(8,128)} %get-tuple-element.87.raw, bf16[1024,1024]{1,0:T(8,128)(2,1)} %broadcast_select_fusion.hits, f32[1024,128]{1,0:T(8,128)} %get-tuple-element.88.stats, f32[1,1024]{1,0:T(1,128)} %and_select_fusion.weight, ...), custom_call_target="tpu_custom_call" | custom-call | bytes 113127680 | tf_op jit(solution)/shard_map/branch_rows/pallas_call | solution.py:300
  374.0 2.5 fusion.130
  376.5 1.7 convolution_convert_fusion.1
  382.2 1.6 fusion.45
  384.3 2.6 multiply_reduce_fusion
  386.9 1.8 multiply_convert_fusion
  388.7 2.4 fusion.44
  393.0 1.5 fusion.134.refs_3_
  398.1 1.9 fusion.36
  402.7 1.4 fusion.77.refs_0_
  405.5 1.4 fusion.73.refs_2_
  406.9 36.7 %fold.1 = (f32[1,1]{1,0:T(1,128)}, f32[1,1]{1,0:T(1,128)}, f32[8,32,128]{2,1,0:T(8,128)}, f32[8,32,128]{2,1,0:T(8,128)}, f32[8,32,128]{2,1,0:T(8,128)}) custom-call(f32[1024,128]{1,0:T(8,128)} %fusion.77.refs_0_, f32[1024,128]{1,0:T(8,128)} %fusion.75.refs_1_, f32[1024,128]{1,0:T(8,128)} %fusion.73.refs_2_, f32[1024,128]{1,0:T(8,128)} %fusion.134.refs_3_, ...), custom_call_target="tpu_custom_call" | custom-call | bytes 103936264 | tf_op jit(solution)/shard_map/fold/pallas_call | solution.py:300
  444.9 1.6 copy.49
  446.5 1.6 copy.50
  448.1 1.6 copy.51
  (144 shorter events, 31.2 us)
Async XLA Ops:
  7.2 113.0 %copy-start = (bf16[1024,1024]{1,0:T(8,128)(2,1)S(1)}, bf16[1024,1024]{1,0:T(8,128)(2,1)}, u32[]{:S(2)}) copy-start(bf16[1024,1024]{1,0:T(8,128)(2,1)} %param.36) | copy-start | bytes 6291460
  7.2 129.1 %all-gather.3.cloned.1.call-start = ((), (), s32[]{:S(2)}) async-start(), calls=%async_computation | async-start | bytes 2162688 | tf_op jit(solution)/shard_map/all_gather | solution.py:741
  8.9 208.9 %all-gather.5.cloned.1.call-start = ((), (), s32[]{:S(2)}) async-start(), calls=%async_computation.1 | async-start | bytes 28975104 | tf_op jit(solution)/shard_map/all_gather | solution.py:742
  18.1 17.8 %copy-start.38 = (s32[1,1024]{1,0:T(1,128)S(1)}, s32[1,1024]{1,0:T(1,128)}, u32[]{:S(2)}) copy-start(s32[1,1024]{1,0:T(1,128)} %param.28) | copy-start | bytes 12292
  113.4 28.5 %copy-start.27 = (f32[1024,8]{0,1:T(8,128)}, f32[1024,8]{0,1:T(8,128)S(1)}, u32[]{:S(2)}) copy-start(f32[1024,8]{0,1:T(8,128)S(1)} %get-tuple-element.120) | copy-start | bytes 98308
  113.4 28.5 %copy-start.29 = (f32[1024,8]{0,1:T(8,128)}, f32[1024,8]{0,1:T(8,128)S(1)}, u32[]{:S(2)}) copy-start(f32[1024,8]{0,1:T(8,128)S(1)} %get-tuple-element.121) | copy-start | bytes 98308
  114.6 5.6 %copy-start.39 = (f32[1024]{0:T(1024)S(1)}, f32[1024]{0:T(1024)}, u32[]{:S(2)}) copy-start(f32[1024]{0:T(1024)} %param.35) | copy-start | bytes 12292
  137.9 13.4 %copy-start.26 = (bf16[1,1024,128]{2,1,0:T(8,128)(2,1)}, bf16[1,1024,128]{2,1,0:T(8,128)(2,1)S(1)}, u32[]{:S(2)}) copy-start(bf16[1,1024,128]{2,1,0:T(8,128)(2,1)S(1)} %get-tuple-element.99) | copy-start | bytes 786436
  137.9 3.2 copy-start.8
  138.0 3.5 copy-start.21
  138.0 4.3 copy-start.23
  142.2 2.0 copy-start.9
  142.2 1.9 copy-start.14
  143.5 4.3 copy-start.3
  146.0 3.3 copy-start.2
  149.2 2.5 copy-start.31
  149.2 2.5 copy-start.11
  151.8 2.3 copy-start.7
  308.5 65.5 %copy-start.12 = (bf16[256,1024]{1,0:T(8,128)(2,1)S(1)}, bf16[256,1024]{1,0:T(8,128)(2,1)}, u32[]{:S(2)}) copy-start(bf16[256,1024]{1,0:T(8,128)(2,1)} %param.33) | copy-start | bytes 1572868
  374.0 2.5 copy-start.6
  374.0 5.5 %copy-start.4 = (f32[4,512,512]{1,2,0:T(8,128)S(1)}, f32[4,512,512]{1,2,0:T(8,128)}, u32[]{:S(2)}) copy-start(f32[4,512,512]{1,2,0:T(8,128)} %copy-done.3) | copy-start | bytes 12582916
  380.4 3.4 slice-start
  380.4 1.7 copy-start.10
  380.4 3.9 slice-start.1
  388.7 2.5 copy-start.13
  400.0 1.8 copy-start.32
  400.0 1.8 copy-start.34
  400.0 1.8 copy-start.37
  400.0 2.7 copy-start.22
  400.0 4.1 copy-start.20
  400.0 5.5 %copy-start.24 = (bf16[1,256,128]{2,1,0:T(8,128)(2,1)S(1)}, bf16[1,256,128]{2,1,0:T(8,128)(2,1)}, u32[]{:S(2)}) copy-start(bf16[1,256,128]{2,1,0:T(8,128)(2,1)} %copy-done.23) | copy-start | bytes 196612
  402.7 46.9 %copy-start.1 = (bf16[1024,1024]{1,0:T(8,128)(2,1)S(1)}, bf16[1024,1024]{1,0:T(8,128)(2,1)}, u32[]{:S(2)}) copy-start(bf16[1024,1024]{1,0:T(8,128)(2,1)} %param.36) | copy-start | bytes 6291460
  (12 other events, 13.9 us)
Sparse Core Ops, SparseCore 0:
  11.5 62.7 all-gather.2
  76.2 131.6 all-gather.4

commit v4 on v3

--- a/solution.py
+++ b/solution.py
@@ -168,7 +168,7 @@
     pl.semaphore_wait(barrier, count - 1)
 
 
-def line_sum(count, chunk, own, wires, sems, prepare, emit, greet=True):
+def line_sum(count, chunk, own, wires, sems, prepare, emit, greet=True, follow=None):
     me = lax.axis_index("mp")
     from_low, from_high, to_high, to_low = wires
     up_send, up_recv, down_send, down_recv = sems
@@ -262,6 +262,8 @@
                 + from_high[rows, :].astype(jnp.float32)
             )
             emit(rows, total)
+            if follow is not None:
+                follow(ready)
 
         return carry
 
@@ -281,8 +283,80 @@
     lax.fori_loop(0, chunks, drain, 0)
 
 
+PICK_GROUP = 32
+PICK_ALIGN = 8
+
+
+def pick_kernel(spots, places, table, out, held, sems):
+    rows = out.shape[0]
+    vocab = table.shape[0]
+    span = PICK_GROUP * PICK_ALIGN
+
+    def start(group, carry):
+        def one(token, carry):
+            at = group * PICK_GROUP + token
+            row = jnp.clip(spots[at], 0, vocab - 1)
+            base = pl.multiple_of(row - lax.rem(row, PICK_ALIGN), PICK_ALIGN)
+            pltpu.make_async_copy(
+                table.at[pl.ds(base, PICK_ALIGN)],
+                held.at[pl.ds(pl.multiple_of(at * PICK_ALIGN, PICK_ALIGN), PICK_ALIGN)],
+                sems.at[group],
+            ).start()
+            return carry
+
+        return lax.fori_loop(0, PICK_GROUP, one, carry, unroll=8)
+
+    lax.fori_loop(0, rows // PICK_GROUP, start, 0)
+
+    def choose(group, carry):
+        block = held.at[pl.ds(pl.multiple_of(group * span, span), span)]
+        pltpu.make_async_copy(table.at[pl.ds(0, span)], block, sems.at[group]).wait()
+        here = line_chunk(group, PICK_GROUP)
+        place = places[here, :]
+        inside = (place >= 0) & (place < vocab)
+        token = lax.broadcasted_iota(jnp.int32, (PICK_GROUP, 1), 0)
+        wanted = jnp.where(
+            inside, token * PICK_ALIGN + lax.rem(jnp.clip(place, 0, vocab - 1), PICK_ALIGN), -1
+        )
+        column = lax.broadcasted_iota(jnp.int32, (PICK_GROUP, span), 1)
+        chosen = jnp.where(column == wanted, 1.0, 0.0).astype(jnp.bfloat16)
+        out[here, :] = jnp.dot(
+            chosen, block[...], preferred_element_type=jnp.float32
+        ).astype(jnp.bfloat16)
+        return carry
+
+    lax.fori_loop(0, rows // PICK_GROUP, choose, 0)
+
+
+def pick_call(spots, table, name):
+    rows = spots.shape[0]
+    width = table.shape[1]
+    return pl.pallas_call(
+        pick_kernel,
+        name=name,
+        in_specs=[
+            pl.BlockSpec(memory_space=pltpu.SMEM),
+            pl.BlockSpec(memory_space=pltpu.VMEM),
+            pl.BlockSpec(memory_space=pl.ANY),
+        ],
+        out_specs=pl.BlockSpec(memory_space=pltpu.VMEM),
+        out_shape=jax.ShapeDtypeStruct((rows, width), jnp.bfloat16),
+        scratch_shapes=[
+            pltpu.VMEM((rows * PICK_ALIGN, width), jnp.bfloat16),
+            pltpu.SemaphoreType.DMA((rows // PICK_GROUP,)),
+        ],
+        compiler_params=pltpu.CompilerParams(vmem_limit_bytes=VMEM_LIMIT),
+        cost_estimate=pl.CostEstimate(
+            flops=2 * rows * PICK_GROUP * PICK_ALIGN * width,
+            bytes_accessed=2 * rows * PICK_ALIGN * width,
+            transcendentals=0,
+        ),
+    )(spots, spots.reshape(rows, 1), table)
+
+
 LINE_CHUNK = 32
 LINE_LAG = 3
+WORK_ROWS = 256
 
 
 def line_scratch(length, width):
@@ -292,7 +366,7 @@
     ] * 4
 
 
-def line_call(kernel, name, collective_id, outs, scratch, operands, flops=0):
+def line_call(kernel, name, collective_id, outs, scratch, operands, flops=0, spaces=()):
     size = sum(o.size * o.dtype.itemsize for o in operands) + sum(
         o.size * o.dtype.itemsize for o in outs
     )
@@ -301,7 +375,8 @@
         kernel,
         name=name,
         out_shape=outs,
-        in_specs=[vmem] * len(operands),
+        in_specs=[vmem] * (len(operands) - len(spaces))
+        + [pl.BlockSpec(memory_space=space) for space in spaces],
         out_specs=[vmem] * len(outs),
         scratch_shapes=scratch,
         compiler_params=pltpu.CompilerParams(
@@ -313,16 +388,63 @@
     )(*operands)
 
 
-def start_kernel(count, part, gain, shift, rows_out, attn_out, ffn_out, *scratch):
+def start_kernel(
+    count,
+    part,
+    gain,
+    shift,
+    bias,
+    w_qkv,
+    w_in,
+    w_down,
+    rows_out,
+    attn_out,
+    base_out,
+    ffn_out,
+    *scratch,
+):
+    normed, held_qkv, held_in, held_down, sems = scratch[8:]
+    loads = [
+        pltpu.make_async_copy(src, dst, sems.at[slot])
+        for slot, (src, dst) in enumerate(
+            ((w_qkv, held_qkv), (w_in, held_in), (w_down, held_down))
+        )
+    ]
+    for load in loads:
+        load.start()
+
     def emit(rows, total):
         rows_out[rows, :] = total.astype(jnp.bfloat16)
         centre = total - jnp.mean(total, -1, keepdims=True)
         spread = jnp.mean(centre * centre, -1, keepdims=True)
         base = centre * lax.rsqrt(spread + NORM_EPS)
         attn_out[rows, :] = (base * gain[0:1, :] + shift[0:1, :]).astype(jnp.bfloat16)
-        ffn_out[rows, :] = (base * gain[1:2, :] + shift[1:2, :]).astype(jnp.bfloat16)
-
-    line_sum(count, LINE_CHUNK, part, scratch[:4], scratch[4:], None, emit)
+        normed[rows, :] = (base * gain[1:2, :] + shift[1:2, :]).astype(jnp.bfloat16)
+
+    per = WORK_ROWS // LINE_CHUNK
+
+    def follow(ready):
+        @pl.when(ready == per - 1)
+        def _():
+            for load in loads:
+                load.wait()
+
+        @pl.when(lax.rem(ready, per) == per - 1)
+        def _():
+            rows = line_chunk(ready // per, WORK_ROWS)
+            base_out[rows, :] = jnp.dot(
+                attn_out[rows, :], held_qkv[...], preferred_element_type=jnp.float32
+            )
+            pre = (
+                jnp.dot(normed[rows, :], held_in[...], preferred_element_type=jnp.float32)
+                + bias[...]
+            )
+            hidden = (0.5 * pre * (1.0 + lax.erf(pre * 0.5**0.5))).astype(jnp.bfloat16)
+            ffn_out[rows, :] = jnp.dot(
+                hidden, held_down[...], preferred_element_type=jnp.float32
+            ).astype(jnp.bfloat16)
+
+    line_sum(count, LINE_CHUNK, part, scratch[:4], scratch[4:8], None, emit, follow=follow)
 
 
 def resid_kernel(count, part, start, gain, shift, resid_out, final_out, *scratch):
@@ -335,7 +457,9 @@
     line_sum(count, LINE_CHUNK, part, scratch[:4], scratch[4:], None, emit)
 
 
-def branch_kernel(count, raw, hits, stats, weight, resid, gain, out, loss_out, *scratch):
+def branch_kernel(
+    count, raw, hits, stats, resid, gain, prompts, totals, out, loss_out, *scratch
+):
     own, note_send, note_recv, scales, note_out, note_in = scratch[8:]
     me = lax.axis_index("mp")
     rows_all = raw.shape[0]
@@ -361,7 +485,11 @@
     total = sum(part[1:2, :] * jnp.exp(part[0:1, :] - top) for part in others)
     found = sum(part[2:3, :] for part in others)
     spread_row = top + jnp.log(total)
-    share = weight[...]
+    amount = sum(totals[e] - prompts[e] for e in range(prompts.shape[0]))
+    example = lax.axis_index("dp")
+    position = lax.broadcasted_iota(jnp.int32, (1, rows_all), 1)
+    keep = (position >= prompts[example] - 1) & (position < totals[example] - 1)
+    share = jnp.where(keep, 1.0 / jnp.broadcast_to(amount, (1, rows_all)).astype(jnp.float32), 0.0)
     loss_out[...] = (spread_row - found) * share
     factor = jnp.exp(mine[0:1, :] - spread_row) * share
     pair = jnp.concatenate([factor, share, jnp.zeros((126, rows_all), jnp.float32)], 0)
@@ -747,37 +875,37 @@
     local_heads = HEADS // group_count
     group_width = local_heads * HD
     flat_ids = token_ids.reshape(rows)
-    relative = flat_ids - group_index * width
-    inside = (relative >= 0) & (relative < width)
-    picked = jnp.where(
-        inside[:, None], embedding[jnp.clip(relative, 0, width - 1)].astype(jnp.float32), 0.0
-    )
+    picked = pick_call(flat_ids - group_index * width, embedding, "pick_start")
     shape_low = jax.ShapeDtypeStruct((rows, D), jnp.bfloat16)
     shape_wide = jax.ShapeDtypeStruct((rows, D), jnp.float32)
-    start_rows, normed_attn, normed_ffn = line_call(
+    start_rows, normed_attn, base, ffn_part = line_call(
         functools.partial(start_kernel, group_count),
         "start_rows",
         0,
-        [shape_low] * 3,
-        line_scratch(rows, D),
-        [picked.astype(jnp.bfloat16), ln_gain, ln_bias],
-    )
-    leading_example = lax.axis_index("dp") * examples
-    prompts = lax.dynamic_slice_in_dim(prompt_len, leading_example, examples)
-    totals = lax.dynamic_slice_in_dim(example_len, leading_example, examples)
-    position = jnp.arange(length)
-    keep = (position[None, :] >= prompts[:, None] - 1) & (position[None, :] < totals[:, None] - 1)
-    count = jnp.sum(example_len - prompt_len).astype(jnp.float32)
-    row_weight = keep.reshape(rows).astype(jnp.float32) / count
+        [
+            shape_low,
+            shape_low,
+            jax.ShapeDtypeStruct((rows, w_qkv.shape[1]), jnp.float32),
+            shape_low,
+        ],
+        line_scratch(rows, D)
+        + [
+            pltpu.VMEM((rows, D), jnp.bfloat16),
+            pltpu.VMEM(w_qkv.shape, jnp.bfloat16),
+            pltpu.VMEM(w_in.shape, jnp.bfloat16),
+            pltpu.VMEM(w_down.shape, jnp.bfloat16),
+            pltpu.SemaphoreType.DMA((3,)),
+        ],
+        [picked, ln_gain, ln_bias, b_in.reshape(1, -1), w_qkv, w_in, w_down],
+        spaces=(pl.ANY,) * 3,
+    )
     target = jnp.roll(token_ids, -1, axis=1).reshape(rows)
     inner = jnp.dot(
         normed_attn,
         jnp.concatenate([adapters[0], adapters[1], adapters[2]], 1),
         preferred_element_type=jnp.float32,
     ).astype(jnp.bfloat16)
-    base = jnp.dot(normed_attn, w_qkv, preferred_element_type=jnp.float32).reshape(
-        rows, local_heads, 3, HD
-    )
+    base = base.reshape(rows, local_heads, 3, HD)
     adapter_rows = [
         lax.dynamic_slice_in_dim(
             adapters[3 + selector_index], group_index * group_width, group_width, 0
@@ -807,13 +935,10 @@
     context = context_here.reshape(rows, group_width)
     out_rows = lax.dynamic_slice_in_dim(adapters[6], group_index * group_width, group_width, 0)
     inner_out = jnp.dot(context, out_rows, preferred_element_type=jnp.float32).astype(jnp.bfloat16)
-    hidden = jax.nn.gelu(
-        jnp.dot(normed_ffn, w_in, preferred_element_type=jnp.float32) + b_in, approximate=False
-    ).astype(jnp.bfloat16)
     partial_value = (
         jnp.dot(context, w_out, preferred_element_type=jnp.float32)
         + jnp.einsum("lr,dr->ld", inner_out, adapters[7], preferred_element_type=jnp.float32)
-        + jnp.dot(hidden, w_down, preferred_element_type=jnp.float32)
+        + ffn_part.astype(jnp.float32)
     )
     resid, final_rows = line_call(
         functools.partial(resid_kernel, group_count),
@@ -824,10 +949,7 @@
         [partial_value.astype(jnp.bfloat16), start_rows, ln_gain, ln_bias],
     )
     goal = target - group_index * vocab_local
-    near = (goal >= 0) & (goal < vocab_local)
-    hits = jnp.where(near[:, None], head_rows[jnp.clip(goal, 0, vocab_local - 1)], 0.0).astype(
-        jnp.bfloat16
-    )
+    hits = pick_call(goal, head_rows, "pick_target")
     raw_grad, stats = loss_call(final_rows, head_rows, hits)
     branch_grad, losses = line_call(
         functools.partial(branch_kernel, group_count),
@@ -843,7 +965,8 @@
             pltpu.SemaphoreType.DMA((group_count,)),
             pltpu.SemaphoreType.DMA((group_count,)),
         ],
-        [raw_grad, hits, stats, row_weight.reshape(1, rows), resid, ln_gain],
+        [raw_grad, hits, stats, resid, ln_gain, prompt_len, example_len],
+        spaces=(pltpu.SMEM,) * 2,
     )
     inner_out_grad = jnp.dot(branch_grad, adapters[7], preferred_element_type=jnp.float32).astype(
         jnp.bfloat16

time: 464 us -> 465 us (level)
  Pallas kernels: 305 us -> 376 us
  local copies, waits for them, and re-layouts: 48.7 us -> 16.9 us
  matrix products: 64.2 us -> 39.4 us
  other arithmetic: 19.6 us -> 13.1 us
    pallas_call x4 -> x6, Pallas kernels: 234 us -> 304 us  [the longest x4 237 us: line_call(): pl.pallas_call(kernel, name=name, out_shape=outs, in_specs=[vmem] * (len(...]
    gather x2 -> x0, local copies, waits for them, and re-layouts: 34.8 us -> none  [the longest x1 17.7 us: per_device(): embedding[jnp.clip(relative, 0, width - 1)].astype(jnp.float32)]
    dot_general x2 -> x0, matrix products: 21.6 us -> none  [the longest x1 16.1 us: per_device(): jnp.dot(hidden, w_down, preferred_element_type=jnp.float32)]
  transfers between devices with their start and end apart: 2 -> 2, of which waited for: 0 -> 0; matrix products, arithmetic and copies ran while one was open for 16% -> 6% of each run, Pallas kernels for 29% -> 36%
where the time goes in v4:
time: 465 us; the launch traced here: 464 us
  Pallas kernels  376 us (81%)
  matrix products  39.4 us (8%)
  between operations  18.5 us (4%)
  local copies, waits for them, and re-layouts  16.9 us (4%)
  other arithmetic  13.1 us (3%)
    pallas_call x4, Pallas kernels, line_call(): pl.pallas_call(kernel, name=name, out_shape=outs, in_specs=[vmem] * (len(...  237 us
    pallas_call x1, Pallas kernels, loss_call(): pl.pallas_call(functools.partial(loss_kernel, vocab, tile), name='loss',...  71.6 us
    pallas_call x2, Pallas kernels, pick_call(): pl.pallas_call(pick_kernel, name=name, in_specs=[pl.BlockSpec(memory_spac...  67.1 us
  transfers between devices with their start and end apart: 2, of which 0 were waited for; matrix products, arithmetic and copies ran while one was open for 6% of the time, Pallas kernels for 36%

profile of v4, /device:TPU:0, one launch (start us, length us, event | category | flops | bytes accessed | tf_op | source)
XLA Modules:
  0.0 464.4 jit_solution(15288783791301153585)
XLA Ops:
  7.2 1.6 convert_element_type.83
  9.6 1.2 slice.245
  15.7 33.8 %pick_start.1.part = bf16[1024,1024]{1,0:T(8,128)(2,1)} custom-call(s32[1024]{0:T(1024)} %bitcast.194, s32[1024,1]{1,0:T(8,128)} %copy.28.places, bf16[12576,1024]{1,0:T(8,128)(2,1)} %table.1), custom_call_target="tpu_custom_call" | custom-call | flops 536870912 | bytes 16777216 | tf_op jit(solution)/shard_map/pick_start/pallas_call | solution.py:334
  49.5 73.6 %start_rows.1 = (bf16[1024,1024]{1,0:T(8,128)(2,1)}, bf16[1024,1024]{1,0:T(8,128)(2,1)}, f32[1024,768]{1,0:T(8,128)}, bf16[1024,1024]{1,0:T(8,128)(2,1)}) custom-call(bf16[1024,1024]{1,0:T(8,128)(2,1)} %pick_start.1.part, f32[3,1024]{1,0:T(4,128)} %gain.5, f32[3,1024]{1,0:T(4,128)} %shift.3, f32[1,1024]{1,0:T(1,128)} %bitcast.195, bf16[1024,768]{1,0:T(8,128)(2,1)} %w_qkv.1, ...), custom_call_target="tpu_custom_call" | custom-call | bytes 117330176 | tf_op jit(solution)/shard_map/start_rows/pallas_call | solution.py:374
  123.1 3.7 copy.29
  126.8 1.3 add_subtract_fusion
  129.1 1.2 iota_compare_fusion
  130.3 1.6 fusion.81
  132.0 1.2 convolution_convert_fusion
  137.2 1.8 fusion.83
  139.0 1.9 fusion
  142.2 2.3 fusion.34
  146.6 3.0 add_convert_fusion.part
  149.7 60.0 %resid_rows.1 = (f32[1024,1024]{1,0:T(8,128)}, bf16[1024,1024]{1,0:T(8,128)(2,1)}) custom-call(bf16[1024,1024]{1,0:T(8,128)(2,1)} %add_convert_fusion.part, bf16[1024,1024]{1,0:T(8,128)(2,1)} %get-tuple-element.87.start, f32[3,1024]{1,0:T(4,128)} %gain.5, f32[3,1024]{1,0:T(4,128)} %shift.3), custom_call_target="tpu_custom_call" | custom-call | bytes 110510336 | tf_op jit(solution)/shard_map/resid_rows/pallas_call | solution.py:374
  209.7 33.3 %pick_target.1.hits = bf16[1024,1024]{1,0:T(8,128)(2,1)} custom-call(s32[1024]{0:T(1024)} %bitcast.193, s32[1024,1]{1,0:T(8,128)} %copy.34.places, bf16[12576,1024]{1,0:T(8,128)(2,1)} %all-gather.5.cloned.1.call-done.table.ahead.behind), custom_call_target="tpu_custom_call" | custom-call | flops 536870912 | bytes 16777216 | tf_op jit(solution)/shard_map/pick_target/pallas_call | solution.py:334
  243.0 71.6 %loss.1 = (f32[1024,1024]{1,0:T(8,128)}, f32[1024,128]{1,0:T(8,128)}) custom-call(bf16[1024,1024]{1,0:T(8,128)(2,1)} %get-tuple-element.88.values, bf16[12576,1024]{1,0:T(8,128)(2,1)} %all-gather.5.cloned.1.call-done.table.ahead.behind, bf16[12576,1024]{1,0:T(8,128)(2,1)} %all-gather.5.cloned.1.call-done.table.ahead.behind, bf16[1024,1024]{1,0:T(8,128)(2,1)} %pick_target.1.hits), custom_call_target="tpu_custom_call" | custom-call | flops 52747567104 | bytes 51511296 | tf_op jit(solution)/shard_map/loss/pallas_call | solution.py:584
  314.7 66.3 %branch_rows.1 = (bf16[1024,1024]{1,0:T(8,128)(2,1)}, f32[1,1024]{1,0:T(1,128)}) custom-call(f32[1024,1024]{1,0:T(8,128)} %get-tuple-element.89.raw, bf16[1024,1024]{1,0:T(8,128)(2,1)} %pick_target.1.hits, f32[1024,128]{1,0:T(8,128)} %get-tuple-element.90.stats, f32[1024,1024]{1,0:T(8,128)} %get-tuple-element.91.resid, f32[3,1024]{1,0:T(4,128)} %gain.5, ...), custom_call_target="tpu_custom_call" | custom-call | bytes 113123648 | tf_op jit(solution)/shard_map/branch_rows/pallas_call | solution.py:374
  381.0 3.3 fusion.89.refs_3_
  385.1 2.0 convolution_convert_fusion.1
  388.1 1.4 fusion.26
  390.4 1.7 fusion.22
  394.9 1.2 multiply_convert_fusion.1
  397.4 2.6 multiply_reduce_fusion
  400.0 2.0 multiply_convert_fusion
  402.0 1.4 fusion.30
  408.0 1.4 fusion.59.refs_2_
  409.4 1.4 fusion.61.refs_1_
  410.8 1.4 fusion.63.refs_0_
  412.3 37.0 %fold.1 = (f32[1,1]{1,0:T(1,128)}, f32[1,1]{1,0:T(1,128)}, f32[8,32,128]{2,1,0:T(8,128)}, f32[8,32,128]{2,1,0:T(8,128)}, f32[8,32,128]{2,1,0:T(8,128)}) custom-call(f32[1024,128]{1,0:T(8,128)} %fusion.63.refs_0_, f32[1024,128]{1,0:T(8,128)} %fusion.61.refs_1_, f32[1024,128]{1,0:T(8,128)} %fusion.59.refs_2_, f32[1024,128]{1,0:T(8,128)} %fusion.89.refs_3_, ...), custom_call_target="tpu_custom_call" | custom-call | bytes 103936264 | tf_op jit(solution)/shard_map/fold/pallas_call | solution.py:374
  450.6 1.6 copy.52
  452.2 1.6 copy.53
  453.8 1.6 copy.54
  (133 shorter events, 24.8 us)
Async XLA Ops:
  7.2 137.8 %copy-start = (bf16[256,1024]{1,0:T(8,128)(2,1)S(1)}, bf16[256,1024]{1,0:T(8,128)(2,1)}, u32[]{:S(2)}) copy-start(bf16[256,1024]{1,0:T(8,128)(2,1)} %param.33) | copy-start | bytes 1572868
  7.2 7.9 %copy-start.37 = (s32[1,1024]{1,0:T(1,128)S(1)}, s32[1,1024]{1,0:T(1,128)}, u32[]{:S(2)}) copy-start(s32[1,1024]{1,0:T(1,128)} %param.28) | copy-start | bytes 12292
  7.2 123.1 %all-gather.3.cloned.1.call-start = ((), (), s32[]{:S(2)}) async-start(), calls=%async_computation | async-start | bytes 2162688 | tf_op jit(solution)/shard_map/all_gather | solution.py:869
  8.9 200.8 %all-gather.5.cloned.1.call-start = ((), (), s32[]{:S(2)}) async-start(), calls=%async_computation.1 | async-start | bytes 28975104 | tf_op jit(solution)/shard_map/all_gather | solution.py:870
  123.0 9.0 %copy-start.4 = (bf16[1024,1024]{1,0:T(8,128)(2,1)S(1)}, bf16[1024,1024]{1,0:T(8,128)(2,1)}, u32[]{:S(2)}) copy-start(bf16[1024,1024]{1,0:T(8,128)(2,1)} %get-tuple-element.84) | copy-start | bytes 6291460
  129.1 5.8 %copy-start.28 = (f32[1024,8]{0,1:T(8,128)}, f32[1024,8]{0,1:T(8,128)S(1)}, u32[]{:S(2)}) copy-start(f32[1024,8]{0,1:T(8,128)S(1)} %get-tuple-element.120) | copy-start | bytes 98308
  129.1 5.8 %copy-start.30 = (f32[1024,8]{0,1:T(8,128)}, f32[1024,8]{0,1:T(8,128)S(1)}, u32[]{:S(2)}) copy-start(f32[1024,8]{0,1:T(8,128)S(1)} %get-tuple-element.121) | copy-start | bytes 98308
  131.9 12.6 %copy-start.27 = (bf16[1,1024,128]{2,1,0:T(8,128)(2,1)}, bf16[1,1024,128]{2,1,0:T(8,128)(2,1)S(1)}, u32[]{:S(2)}) copy-start(bf16[1,1024,128]{2,1,0:T(8,128)(2,1)S(1)} %get-tuple-element.99) | copy-start | bytes 786436
  131.9 2.2 copy-start.6
  132.0 2.4 copy-start.22
  132.0 3.2 copy-start.24
  133.3 2.0 copy-start.7
  134.9 1.6 copy-start.12
  135.0 2.1 copy-start.16
  135.0 2.1 copy-start.18
  135.2 2.0 copy-start.9
  136.5 4.3 copy-start.2
  139.0 3.3 copy-start.1
  142.2 2.7 copy-start.32
  144.9 1.7 copy-start.11
  314.7 66.4 %copy-start.15 = (bf16[1024,128]{1,0:T(8,128)(2,1)S(1)}, bf16[1024,128]{1,0:T(8,128)(2,1)}, u32[]{:S(2)}) copy-start(bf16[1024,128]{1,0:T(8,128)(2,1)} %copy-done.14) | copy-start | bytes 786436
  381.0 3.3 copy-start.5
  384.3 2.8 copy-start.33
  384.3 2.8 copy-start.35
  384.3 6.1 %slice-start = ((s8[8388608]{0:T(1024)(128)(4,1)}), s8[4194304]{0:T(1024)(128)(4,1)S(1)}, s32[]{:S(2)}) async-start(s8[8388608]{0:T(1024)(128)(4,1)} %bitcast.162), calls=%async_computation.2 | async-start | bytes 8388608
  385.1 4.5 copy-start.3
  387.1 3.2 slice-start.1
  390.4 1.8 copy-start.8
  394.9 1.7 copy-start.10
  406.2 1.8 copy-start.25
  406.2 3.2 copy-start.21
  407.2 3.6 copy-start.23
  (10 other events, 11.0 us)
Sparse Core Ops, SparseCore 0:
  11.5 61.4 all-gather.2
  74.9 131.5 all-gather.4
